TPU v7x, 32 devices: a whole 2x2x4 slice. The times are simulated.
32 devices in a mesh: rep: 4 (over z), shard: 4 (over y, x), seq: 2 (over core).
Axes of the slice: x: 2, y: 2, z: 4, core: 2. Of those that a mesh axis runs over, the one named last changes fastest.
Arguments:
- tokens_in: bfloat16 [4096, 1024], P(('rep', 'shard', 'seq')), may hold values from -6 to 6
- doc_lengths: int32 [4, 4], P('rep'), may hold values from 1 to 512, 1024 in all within a row
- attn_gain: float32 [1024], replicated, may hold values from 0.25 to 1.75
- w_query: bfloat16 [1024, 1024], P('shard'), may hold values from -0.1875 to 0.1875
- key_weight: bfloat16 [1024, 512], P('shard'), may hold values from -0.1875 to 0.1875
- value_weight: bfloat16 [1024, 512], P('shard'), may hold values from -0.1875 to 0.1875
- w_output: bfloat16 [1024, 1024], P('shard'), may hold values from -2 to 2
- query_norm_gain: float32 [64], replicated, may hold values from 0.5 to 2
- key_norm_gain: float32 [64], replicated, may hold values from 0.5 to 2
- mlp_gain: float32 [1024], replicated, may hold values from 0.25 to 1.75
- w_gate: bfloat16 [4608, 1024], P('shard'), may hold values from -0.1875 to 0.1875
- w_up: bfloat16 [4608, 1024], P('shard'), may hold values from -0.1875 to 0.1875
- w_down: bfloat16 [4608, 1024], P('shard'), may hold values from -0.09375 to 0.09375
- out_grad: bfloat16 [4096, 1024], P(('rep', 'shard', 'seq')), may hold values from -6 to 6
Outputs:
- act_out: float32 [4096, 1024], P(('rep', 'shard', 'seq'))
- in_grad: float32 [4096, 1024], P(('rep', 'shard', 'seq'))
- grad_attn_gain: float32 [1024], replicated
- grad_query: float32 [1024, 1024], P(('shard', 'seq'))
- grad_key: float32 [1024, 512], P(('shard', 'seq'))
- grad_value: float32 [1024, 512], P(('shard', 'seq'))
- grad_output: float32 [1024, 1024], P(('shard', 'seq'))
- grad_query_gain: float32 [64], replicated
- grad_key_gain: float32 [64], replicated
- grad_mlp_gain: float32 [1024], replicated
- grad_gate: float32 [4608, 1024], P(('shard', 'seq'))
- grad_up: float32 [4608, 1024], P(('shard', 'seq'))
- grad_down: float32 [4608, 1024], P(('shard', 'seq'))
Inputs may be any that keep to these rules, and one draw needn't show every extreme that they name: `doc_lengths`: each row sums to 1024, and its largest entry is exactly 512.
All inputs are finite; a program needn't handle non-finite values.
Results may differ from a plain program's by a relative error of at most 0.014.
The roundings to bfloat16 on the way count: a program that leaves them out, or rounds other values in their place, can miss the bound.
Values may be sent and summed in bfloat16 or wider, within the bound.
No kernel may reach another device: no remote copies, remote signals or barrier semaphores. Data moves between devices by JAX's collectives and lax.ppermute only.
A program may use at most 256 MiB of HBM per device.

v0:
```python
import jax
import jax.numpy as jnp
from jax import lax
from jax.sharding import PartitionSpec as P

norm_eps = 1e-05
rope_base = 1000000.0
very_low = -1e30
contract_last = (((1,), (1,)), ((), ()))
contract_first = (((0,), (0,)), ((), ()))


def rms_scale(values):
    return lax.rsqrt(jnp.mean(values * values, axis=-1, keepdims=True) + norm_eps)


def root_mean_backward(normed, factor, gain, upstream):
    scaled = upstream * gain
    return factor * (scaled - normed * jnp.mean(scaled * normed, axis=-1, keepdims=True))


def rope_tables(positions, head_dim):
    half_dim = head_dim // 2
    inverse_freq = rope_base ** (-(jnp.arange(half_dim, dtype=jnp.float32) * 2.0 / head_dim))
    angles = positions.astype(jnp.float32)[:, None] * inverse_freq[None, :]
    return (jnp.cos(angles)[:, None, :], jnp.sin(angles)[:, None, :])


def rotate_pairs(values, cosine_table, sine_values):
    half_dim = values.shape[-1] // 2
    lower_half = values[..., :half_dim]
    upper_half = values[..., half_dim:]
    return jnp.concatenate(
        [
            lower_half * cosine_table - upper_half * sine_values,
            upper_half * cosine_table + lower_half * sine_values,
        ],
        axis=-1,
    )


def rotate_back(grads, cosine_table, sine_values):
    half_dim = grads.shape[-1] // 2
    lower_half = grads[..., :half_dim]
    upper_half = grads[..., half_dim:]
    return jnp.concatenate(
        [
            lower_half * cosine_table + upper_half * sine_values,
            upper_half * cosine_table - lower_half * sine_values,
        ],
        axis=-1,
    )


def doc_info(lengths, positions):
    doc_ends = jnp.cumsum(lengths)
    finished = doc_ends[None, :] <= positions[:, None]
    doc_ids = jnp.sum(finished.astype(jnp.int32), axis=1)
    doc_first = jnp.sum(jnp.where(finished, lengths[None, :], 0), axis=1)
    return (doc_ids, positions - doc_first)


def local(
    tokens_in,
    doc_lengths,
    attn_gain,
    w_query,
    key_weight,
    value_weight,
    w_output,
    query_norm_gain,
    key_norm_gain,
    mlp_gain,
    w_gate,
    w_up,
    w_down,
    out_grad,
):
    row_count = tokens_in.shape[0]
    model_width = tokens_in.shape[1]
    head_dim = query_norm_gain.shape[0]
    query_width = w_query.shape[1]
    kv_width = key_weight.shape[1]
    kv_heads = kv_width // head_dim
    head_grouping = query_width // kv_width
    score_scale = head_dim ** (-0.5)
    rank_count = lax.axis_size("shard") * lax.axis_size("seq")
    group_rows = row_count * rank_count
    first_row = lax.axis_index(("shard", "seq")) * row_count
    key_block = min(512, group_rows)
    block_count = group_rows // key_block
    key_index = jnp.arange(group_rows, dtype=jnp.int32)
    key_docs, key_offset = doc_info(doc_lengths[0], key_index)
    query_index = first_row + jnp.arange(row_count, dtype=jnp.int32)
    query_docs = lax.dynamic_slice_in_dim(key_docs, first_row, row_count)
    query_offset = lax.dynamic_slice_in_dim(key_offset, first_row, row_count)
    cosine_table, sine_values = rope_tables(query_offset, head_dim)
    x_float = tokens_in.astype(jnp.float32)
    norm_one = rms_scale(x_float)
    x_hat = x_float * norm_one
    normalized_input = (x_hat * attn_gain).astype(jnp.bfloat16)
    pieces = (
        lax.all_gather(w_query, "shard", axis=0, tiled=True),
        lax.all_gather(key_weight, "shard", axis=0, tiled=True),
        lax.all_gather(value_weight, "shard", axis=0, tiled=True),
    )
    in_cols = normalized_input
    queries, key_proj, value_proj = tuple(
        (jnp.dot(in_cols, weight, preferred_element_type=jnp.float32) for weight in pieces)
    )
    query_heads = queries.reshape(row_count, query_width // head_dim, head_dim)
    query_norm = rms_scale(query_heads)
    query_normalized = query_heads * query_norm
    query_rotated = rotate_pairs(
        query_normalized * query_norm_gain, cosine_table, sine_values
    ).astype(jnp.bfloat16)
    key_head_rows = key_proj.reshape(row_count, kv_heads, head_dim)
    key_head_norm = rms_scale(key_head_rows)
    key_normalized = key_head_rows * key_head_norm
    key_rot = rotate_pairs(key_normalized * key_norm_gain, cosine_table, sine_values).astype(
        jnp.bfloat16
    )
    value_rows = value_proj.astype(jnp.bfloat16)
    key_all, value_all = (
        lax.all_gather(key_rot.reshape(row_count, kv_width), ("shard", "seq"), axis=0, tiled=True),
        lax.all_gather(value_rows, ("shard", "seq"), axis=0, tiled=True),
    )
    query_grouped = query_rotated.reshape(row_count, kv_heads, head_grouping, head_dim)

    def block_mask(offset, span_rows):
        docs_here = lax.dynamic_slice_in_dim(key_docs, offset, span_rows)
        index_here = offset + jnp.arange(span_rows, dtype=jnp.int32)
        return (query_docs[:, None] == docs_here[None, :]) & (
            index_here[None, :] <= query_index[:, None]
        )

    def block_scores(offset, span_rows, allowed):
        key_rows = lax.dynamic_slice_in_dim(key_all, offset, span_rows, 0).reshape(
            span_rows, kv_heads, head_dim
        )
        value_block = lax.dynamic_slice_in_dim(value_all, offset, span_rows, 0).reshape(
            span_rows, kv_heads, head_dim
        )
        scores = (
            jnp.einsum(
                "tgjd,rgd->gjtr", query_grouped, key_rows, preferred_element_type=jnp.float32
            )
            * score_scale
        )
        return (jnp.where(allowed, scores, very_low), key_rows, value_block)

    def total_block(block_index, running):
        offset = block_index * key_block
        allowed = block_mask(offset, key_block)

        def total_accumulate(softmax_state):
            row_high, row_total = softmax_state
            scores, key_rows, value_block = block_scores(offset, key_block, allowed)
            new_high = jnp.maximum(row_high, jnp.max(scores, axis=-1))
            exp_scores = jnp.where(allowed, jnp.exp(scores - new_high[..., None]), 0.0)
            row_total = row_total * jnp.exp(row_high - new_high) + jnp.sum(exp_scores, axis=-1)
            return (new_high, row_total)

        return lax.cond(
            jnp.any(allowed), total_accumulate, lambda softmax_state: softmax_state, running
        )

    softmax_init = (
        jnp.full((kv_heads, head_grouping, row_count), very_low, jnp.float32),
        jnp.zeros((kv_heads, head_grouping, row_count), jnp.float32),
    )
    row_high, row_total = lax.fori_loop(0, block_count, total_block, softmax_init)
    log_total = row_high + jnp.log(row_total)

    def mix_block(block_index, weighted):
        offset = block_index * key_block
        allowed = block_mask(offset, key_block)

        def mix_accumulate(current):
            scores, key_rows, value_block = block_scores(offset, key_block, allowed)
            attn_prob = jnp.where(allowed, jnp.exp(scores - log_total[..., None]), 0.0).astype(
                jnp.bfloat16
            )
            return current + jnp.einsum(
                "gjtr,rgd->gjtd", attn_prob, value_block, preferred_element_type=jnp.float32
            )

        return lax.cond(jnp.any(allowed), mix_accumulate, lambda current: current, weighted)

    weighted = lax.fori_loop(
        0,
        block_count,
        mix_block,
        jnp.zeros((kv_heads, head_grouping, row_count, head_dim), jnp.float32),
    )
    head_mixture = (
        weighted.transpose(2, 0, 1, 3).reshape(row_count, query_width).astype(jnp.bfloat16)
    )
    attn_part = lax.dot_general(
        head_mixture,
        lax.all_gather(w_output, "shard", axis=0, tiled=True),
        contract_last,
        preferred_element_type=jnp.float32,
    )
    residual = x_float + attn_part
    norm_two = rms_scale(residual)
    resid_hat = residual * norm_two
    normed_mid = (resid_hat * mlp_gain).astype(jnp.bfloat16)
    gate_rows = lax.all_gather(w_gate, "shard", axis=0, tiled=True)
    up_rows = lax.all_gather(w_up, "shard", axis=0, tiled=True)
    down_rows = lax.all_gather(w_down, "shard", axis=0, tiled=True)
    gate_part = lax.dot_general(
        normed_mid, gate_rows, contract_last, preferred_element_type=jnp.float32
    )
    up_part = lax.dot_general(
        normed_mid, up_rows, contract_last, preferred_element_type=jnp.float32
    )
    hidden_part = (gate_part * jax.nn.sigmoid(gate_part) * up_part).astype(jnp.bfloat16)
    mlp_sum = jnp.dot(hidden_part, down_rows, preferred_element_type=jnp.float32)
    mlp_gate_store = gate_part
    mlp_up_store = up_part
    hidden_store = hidden_part
    mlp_sum, gate_store, up_store, hidden_store = (
        mlp_sum,
        mlp_gate_store,
        mlp_up_store,
        hidden_store,
    )
    act_out = residual + mlp_sum
    grad_float = out_grad.astype(jnp.float32)
    gate_rows = lax.all_gather(w_gate, "shard", axis=0, tiled=True)
    up_rows = lax.all_gather(w_up, "shard", axis=0, tiled=True)
    down_rows = lax.all_gather(w_down, "shard", axis=0, tiled=True)
    span_rows = gate_rows.shape[0]
    gate_part = gate_store
    up_part = up_store
    grad_hidden = lax.dot_general(
        out_grad, down_rows, contract_last, preferred_element_type=jnp.float32
    )
    gate_sig = jax.nn.sigmoid(gate_part)
    gate_grad = (grad_hidden * up_part * gate_sig * (1.0 + gate_part * (1.0 - gate_sig))).astype(
        jnp.bfloat16
    )
    up_grad = (grad_hidden * gate_part * gate_sig).astype(jnp.bfloat16)
    grad_mid = jnp.dot(gate_grad, gate_rows, preferred_element_type=jnp.float32) + jnp.dot(
        up_grad, up_rows, preferred_element_type=jnp.float32
    )
    gate_grad_store = gate_grad
    up_grad_store = up_grad
    grad_mid, gate_grad_store, up_grad_store = (grad_mid, gate_grad_store, up_grad_store)
    grad_resid = grad_float + root_mean_backward(resid_hat, norm_two, mlp_gain, grad_mid)
    mlp_gain_part = jnp.sum(grad_mid * resid_hat, axis=0)
    grad_resid_b = grad_resid.astype(jnp.bfloat16)
    resid_cols = grad_resid_b
    mixing_gradient = jnp.dot(
        resid_cols,
        lax.all_gather(w_output, "shard", axis=0, tiled=True),
        preferred_element_type=jnp.float32,
    ).astype(jnp.bfloat16)
    mix_grouped = mixing_gradient.reshape(row_count, kv_heads, head_grouping, head_dim)
    delta_row_values = jnp.sum(
        (mixing_gradient.astype(jnp.float32) * head_mixture.astype(jnp.float32)).reshape(
            row_count, kv_heads, head_grouping, head_dim
        ),
        axis=-1,
    ).transpose(1, 2, 0)

    def score_grads(offset, span_rows, allowed):
        scores, key_rows, value_block = block_scores(offset, span_rows, allowed)
        attn_prob = jnp.where(allowed, jnp.exp(scores - log_total[..., None]), 0.0)
        grad_prob = jnp.einsum(
            "tgjd,rgd->gjtr", mix_grouped, value_block, preferred_element_type=jnp.float32
        )
        grad_score = (attn_prob * (grad_prob - delta_row_values[..., None])).astype(jnp.bfloat16)
        return (attn_prob, grad_score, key_rows)

    def query_pass(block_index, grad_sum):
        offset = block_index * key_block
        allowed = block_mask(offset, key_block)

        def query_accumulate(current):
            attn_prob, grad_score, key_rows = score_grads(offset, key_block, allowed)
            return current + score_scale * jnp.einsum(
                "gjtr,rgd->tgjd", grad_score, key_rows, preferred_element_type=jnp.float32
            )

        return lax.cond(jnp.any(allowed), query_accumulate, lambda current: current, grad_sum)

    query_rot_grad = lax.fori_loop(
        0,
        block_count,
        query_pass,
        jnp.zeros((row_count, kv_heads, head_grouping, head_dim), jnp.float32),
    )

    def one_block(start_row):
        allowed = block_mask(start_row, key_block)

        def compute(unused):
            attn_prob, grad_score, key_rows = score_grads(start_row, key_block, allowed)
            key_grad = score_scale * jnp.einsum(
                "gjtr,tgjd->rgd", grad_score, query_grouped, preferred_element_type=jnp.float32
            )
            value_grad = jnp.einsum(
                "gjtr,tgjd->rgd",
                attn_prob.astype(jnp.bfloat16),
                mix_grouped,
                preferred_element_type=jnp.float32,
            )
            return jnp.concatenate(
                [key_grad.reshape(key_block, kv_width), value_grad.reshape(key_block, kv_width)],
                axis=1,
            )

        return lax.cond(
            jnp.any(allowed),
            compute,
            lambda unused: jnp.zeros((key_block, 2 * kv_width), jnp.float32),
            0,
        )

    starts = key_block * jnp.arange(
        row_count * lax.axis_size(("shard", "seq")) // key_block, dtype=jnp.int32
    )
    kv_summed = lax.psum_scatter(
        lax.map(one_block, starts).reshape(
            row_count * lax.axis_size(("shard", "seq")), 2 * kv_width
        ),
        ("shard", "seq"),
        scatter_dimension=0,
        tiled=True,
    )
    key_rot_grad = kv_summed[:, :kv_width].reshape(row_count, kv_heads, head_dim)
    value_grad_b = kv_summed[:, kv_width:].astype(jnp.bfloat16)
    key_unrotated = rotate_back(key_rot_grad, cosine_table, sine_values)
    key_gain_part = jnp.sum(key_unrotated * key_normalized, axis=(0, 1))
    key_row_gradient = (
        root_mean_backward(key_normalized, key_head_norm, key_norm_gain, key_unrotated)
        .reshape(row_count, kv_width)
        .astype(jnp.bfloat16)
    )
    query_unrot = rotate_back(
        query_rot_grad.reshape(row_count, query_width // head_dim, head_dim),
        cosine_table,
        sine_values,
    )
    query_gain_part = jnp.sum(query_unrot * query_normalized, axis=(0, 1))
    grad_query_rows = (
        root_mean_backward(query_normalized, query_norm, query_norm_gain, query_unrot)
        .reshape(row_count, query_width)
        .astype(jnp.bfloat16)
    )
    query_rows, key_rows, value_rows_w = lax.all_gather(
        (w_query, key_weight, value_weight), "shard", axis=0, tiled=True
    )
    grad_in_norm = (
        lax.dot_general(
            grad_query_rows, query_rows, contract_last, preferred_element_type=jnp.float32
        )
        + lax.dot_general(
            key_row_gradient, key_rows, contract_last, preferred_element_type=jnp.float32
        )
        + lax.dot_general(
            value_grad_b, value_rows_w, contract_last, preferred_element_type=jnp.float32
        )
    )
    in_grad = grad_resid + root_mean_backward(x_hat, norm_one, attn_gain, grad_in_norm)
    attn_gain_part = jnp.sum(grad_in_norm * x_hat, axis=0)
    grad_attn_gain, grad_mlp_gain, grad_query_gain, grad_key_gain = lax.psum(
        (attn_gain_part, mlp_gain_part, query_gain_part, key_gain_part), ("rep", "shard", "seq")
    )
    attn_grads = jnp.concatenate([grad_query_rows, key_row_gradient, value_grad_b], axis=1)
    d_share = model_width // rank_count
    in_own, resid_own, gate_own, up_own, hidden_own = (
        lax.all_to_all(normalized_input, ("shard", "seq"), split_axis=1, concat_axis=0, tiled=True),
        lax.all_to_all(grad_resid_b, ("shard", "seq"), split_axis=1, concat_axis=0, tiled=True),
        lax.all_to_all(gate_grad_store, ("shard", "seq"), split_axis=1, concat_axis=0, tiled=True),
        lax.all_to_all(up_grad_store, ("shard", "seq"), split_axis=1, concat_axis=0, tiled=True),
        lax.all_to_all(hidden_store, ("shard", "seq"), split_axis=1, concat_axis=0, tiled=True),
    )
    attn_piece = lax.all_gather(attn_grads, ("shard", "seq"), axis=0, tiled=True)
    mix_piece = lax.all_gather(head_mixture, ("shard", "seq"), axis=0, tiled=True)
    mid_piece = lax.all_gather(normed_mid, ("shard", "seq"), axis=0, tiled=True)
    grad_piece = lax.all_gather(out_grad, ("shard", "seq"), axis=0, tiled=True)
    span_rows = attn_piece.shape[0]
    in_cols = in_own
    resid_cols = resid_own
    attn_rows = jnp.concatenate(
        [
            lax.dot_general(
                in_cols, attn_piece, contract_first, preferred_element_type=jnp.float32
            ),
            lax.dot_general(
                resid_cols, mix_piece, contract_first, preferred_element_type=jnp.float32
            ),
        ],
        axis=1,
    )
    mlp_rows = jnp.concatenate(
        [
            lax.dot_general(
                gate_own, mid_piece, contract_first, preferred_element_type=jnp.float32
            ),
            lax.dot_general(up_own, mid_piece, contract_first, preferred_element_type=jnp.float32),
            lax.dot_general(
                hidden_own, grad_piece, contract_first, preferred_element_type=jnp.float32
            ),
        ],
        axis=1,
    )
    group_grads = jnp.concatenate([attn_rows, mlp_rows], axis=0)
    own_grads = lax.psum(group_grads, "rep")
    attn_block_grads = own_grads[:d_share]
    mlp_block_grads = own_grads[d_share:]
    grad_query = attn_block_grads[:, :query_width]
    grad_key = attn_block_grads[:, query_width : query_width + kv_width]
    grad_value = attn_block_grads[:, query_width + kv_width : query_width + 2 * kv_width]
    grad_output = attn_block_grads[:, query_width + 2 * kv_width :]
    grad_gate = mlp_block_grads[:, :model_width]
    grad_up = mlp_block_grads[:, model_width : 2 * model_width]
    grad_down = mlp_block_grads[:, 2 * model_width :]
    return (
        act_out,
        in_grad,
        grad_attn_gain,
        grad_query,
        grad_key,
        grad_value,
        grad_output,
        grad_query_gain,
        grad_key_gain,
        grad_mlp_gain,
        grad_gate,
        grad_up,
        grad_down,
    )


def solution(mesh):
    placed = (
        P(("rep", "shard", "seq"), None),
        P("rep", None),
        P(),
        P("shard", None),
        P("shard", None),
        P("shard", None),
        P("shard", None),
        P(),
        P(),
        P(),
        P("shard", None),
        P("shard", None),
        P("shard", None),
        P(("rep", "shard", "seq"), None),
    )
    return jax.shard_map(
        local,
        mesh=mesh,
        in_specs=placed,
        out_specs=(
            P(("rep", "shard", "seq"), None),
            P(("rep", "shard", "seq"), None),
            P(),
            P(("shard", "seq"), None),
            P(("shard", "seq"), None),
            P(("shard", "seq"), None),
            P(("shard", "seq"), None),
            P(),
            P(),
            P(),
            P(("shard", "seq"), None),
            P(("shard", "seq"), None),
            P(("shard", "seq"), None),
        ),
        check_vma=False,
    )
```

profile of v0, /device:TPU:0, one launch (start us, length us, event | category | flops | bytes accessed | tf_op | source)
XLA Modules:
  0.0 1089.9 jit_solution(5527229661544822959)
XLA Ops:
  12.2 26.9 %all-gather.20.cloned.1.call-done = bf16[1024,512]{1,0:T(8,128)(2,1)} async-done(((bf16[256,512]{1,0:T(8,128)(2,1)}), bf16[1024,512]{1,0:T(8,128)(2,1)}) %all-gather.20.cloned.1.call-update) | async-done | bytes 1048592 | tf_op jit(solution)/shard_map/all_gather | solution.py:105
  41.8 25.7 %all-gather.14.cloned.1.call-done = bf16[1024,512]{1,0:T(8,128)(2,1)} async-done(((bf16[256,512]{1,0:T(8,128)(2,1)}), bf16[1024,512]{1,0:T(8,128)(2,1)}) %all-gather.14.cloned.1.call-update) | async-done | bytes 1048592 | tf_op jit(solution)/shard_map/all_gather | solution.py:104
  73.1 31.4 %all-gather.18.cloned.1.call-done = bf16[1024,1024]{1,0:T(8,128)(2,1)} async-done(((bf16[256,1024]{1,0:T(8,128)(2,1)}), bf16[1024,1024]{1,0:T(8,128)(2,1)}) %all-gather.18.cloned.1.call-update) | async-done | bytes 2097168 | tf_op jit(solution)/shard_map/all_gather | solution.py:103
  107.6 22.6 %all-gather.22.cloned.1.call-done = bf16[1024,512]{1,0:T(8,128)(2,1)} async-done(((bf16[128,512]{1,0:T(8,128)(2,1)}), bf16[1024,512]{1,0:T(8,128)(2,1)}) %all-gather.22.cloned.1.call-update) | async-done | bytes 1048592 | tf_op jit(solution)/shard_map/all_gather | solution.py:126
  131.7 24.3 %all-gather.16.cloned.1.call-done = bf16[1024,512]{0,1:T(8,128)(2,1)} async-done(((bf16[128,512]{0,1:T(8,128)(2,1)}), bf16[1024,512]{0,1:T(8,128)(2,1)}) %all-gather.16.cloned.1.call-update) | async-done | bytes 1048592 | tf_op jit(solution)/shard_map/all_gather | solution.py:125
  156.1 6.2 while.61
  157.6 3.0 conditional.12
  162.3 6.1 while.62
  168.7 24.3 %all-gather.24.cloned.1.call-done = bf16[1024,1024]{1,0:T(8,128)(2,1)} async-done(((bf16[256,1024]{1,0:T(8,128)(2,1)}), bf16[1024,1024]{1,0:T(8,128)(2,1)}) %all-gather.24.cloned.1.call-update) | async-done | bytes 2097168 | tf_op jit(solution)/shard_map/all_gather | solution.py:201
  195.6 95.4 %all-gather.26.cloned.1.call-done = bf16[4608,1024]{1,0:T(8,128)(2,1)} async-done(((bf16[1152,1024]{1,0:T(8,128)(2,1)}), bf16[4608,1024]{1,0:T(8,128)(2,1)}) %all-gather.26.cloned.1.call-update) | async-done | bytes 9437200 | tf_op jit(solution)/shard_map/all_gather | solution.py:209
  291.0 8.3 fusion.85
  299.3 89.8 %all-gather.28.cloned.1.call-done = bf16[4608,1024]{1,0:T(8,128)(2,1)} async-done(((bf16[1152,1024]{1,0:T(8,128)(2,1)}), bf16[4608,1024]{1,0:T(8,128)(2,1)}) %all-gather.28.cloned.1.call-update) | async-done | bytes 9437200 | tf_op jit(solution)/shard_map/all_gather | solution.py:210
  389.1 8.3 fusion.86
  397.4 89.8 %all-gather.30.cloned.1.call-done = bf16[4608,1024]{1,0:T(8,128)(2,1)} async-done(((bf16[1152,1024]{1,0:T(8,128)(2,1)}), bf16[4608,1024]{1,0:T(8,128)(2,1)}) %all-gather.30.cloned.1.call-update) | async-done | bytes 9437200 | tf_op jit(solution)/shard_map/all_gather | solution.py:211
  487.2 9.9 multiply_convert_fusion
  497.1 6.0 fusion.87
  509.7 35.1 %while.64 = (s32[]{:T(128)}, f32[2,512,1024]{2,1,0:T(8,128)}, s32[128]{0:T(128)S(1)}, s32[2]{0:T(128)S(1)}, s32[1024]{0:T(1024)S(1)}, /*index=5*/bf16[1024,512]{...) while((s32[]{:T(128)}, f32[2,512,1024]{2,1,0:T(8,128)}, ...), condition=%wide.region_31.32_spmd.clone, body=%wide.region_27.31_spmd.clone.sunk | while | flops 550503040 | bytes 36934120 | solution.py:326
  514.7 15.1 %conditional.15 = (f32[1,512,1024]{1,2,0:T(8,128)S(1)}) conditional(s32[]{:T(128)} %convert_element_type.210, () %tuple.202, (pred[128,512]{0,1:T(8,128)(4,1)S(1)}, s32[]{:T(128)}, bf16[1024,512]{0,1:T(8,128)(2,1)S(1)}, bf16[128,8,2,64]{0,3,2,1:T(8,128)(2,1)S(1)}, f32[8,2,128]{2,1,0:T(2,128)S(1)}, /*index=5*/bf16[1024,512]{0,1:T(8,128)(2,1)}, ...), branch_computations={%region_29.29_spmd, %region_30.30_spmd} | conditional | flops 550240256 | bytes 28467302 | solution.py:315
  518.2 2.8 fusion.84
  521.0 5.1 fusion.41
  526.2 3.4 fusion.36
  531.6 3.2 constant_dynamic-update-slice_fusion.2
  541.6 3.2 constant_dynamic-update-slice_fusion.2
  549.8 11.1 %while.63 = (s32[]{:T(128)}, f32[128,8,2,64]{0,3,2,1:T(8,128)}, s32[128]{0:T(128)S(1)}, s32[1024]{0:T(1024)S(1)}, bf16[1024,512]{0,1:T(8,128)(2,1)S(1)}, /*index...) while((s32[]{:T(128)}, f32[128,8,2,64]{0,3,2,1:T(8,128)}, ...), condition=%wide.region_25.26_spmd.clone, body=%wide.region_21.25_spmd.clone.sunk | while | flops 410518144 | bytes 13791043 | solution.py:289
  551.4 7.9 conditional.14
  551.5 2.8 fusion.83
  554.4 5.0 fusion.26
  564.1 44.8 %reduce-scatter.2.cloned.1.call-done = f32[128,1024]{1,0:T(8,128)} async-done(((f32[1024,1024]{1,0:T(8,128)}), f32[128,1024]{1,0:T(8,128)}) %reduce-scatter.2.cloned.1.call-update) | async-done | bytes 524304 | tf_op jit(solution)/shard_map/reduce_scatter | solution.py:325
  613.4 3.4 all-to-all-start.1
  618.3 7.7 all-to-all-done.1
  626.7 4.3 all-to-all-start.3
  632.4 20.0 %all-to-all-done.3 = bf16[128,8,576]{0,2,1:T(8,128)(2,1)} async-done(((bf16[128,8,576]{0,2,1:T(8,128)(2,1)}), bf16[128,8,576]{0,2,1:T(8,128)(2,1)}, u32[]{:S(2)}, u32[]{:S(2)}) %all-to-all-start.3) | async-done | bytes 1179680 | tf_op jit(solution)/shard_map/all_to_all | solution.py:378
  652.4 4.5 all-to-all-start.2
  663.3 24.5 %all-gather.36.cloned.1.call-done = bf16[1024,1024]{1,0:T(8,128)(2,1)} async-done(((bf16[128,1024]{1,0:T(8,128)(2,1)}), bf16[1024,1024]{1,0:T(8,128)(2,1)}) %all-gather.36.cloned.1.call-update) | async-done | bytes 2097168 | tf_op jit(solution)/shard_map/all_gather | solution.py:383
  687.8 4.7 fusion.51
  692.5 4.3 all-to-all-start.4
  696.8 4.9 fusion.54
  704.7 11.6 %all-to-all-done.4 = bf16[128,8,576]{0,2,1:T(8,128)(2,1)} async-done(((bf16[128,8,576]{0,2,1:T(8,128)(2,1)}), bf16[128,8,576]{0,2,1:T(8,128)(2,1)}, u32[]{:S(2)}, u32[]{:S(2)}) %all-to-all-start.4) | async-done | bytes 1179680 | tf_op jit(solution)/shard_map/all_to_all | solution.py:379
  716.3 3.4 all-to-all-start
  719.7 3.7 all-gather.38.cloned.1.call-done
  723.4 4.7 fusion.48
  728.2 34.2 %all-gather.32.cloned.1.call-done = bf16[1024,2048]{1,0:T(8,128)(2,1)} async-done(((bf16[128,2048]{1,0:T(8,128)(2,1)}), bf16[1024,2048]{1,0:T(8,128)(2,1)}) %all-gather.32.cloned.1.call-update) | async-done | bytes 4194320 | tf_op jit(solution)/shard_map/all_gather | solution.py:381
  762.4 3.1 fusion.89
  766.0 6.0 maximum_maximum_fusion
  773.0 5.9 convolution_add_fusion.4
  779.1 43.9 %all-reduce = (f32[1024]{0:T(1024)}, f32[64]{0:T(128)}, f32[64]{0:T(128)}, f32[1024]{0:T(1024)}) all-reduce(f32[1024]{0:T(1024)S(1)} %get-tuple-element.870, f32[64]{0:T(128)S(1)} %reduce_sum.172, f32[64]{0:T(128)S(1)} %reduce_sum.175, f32[1024]{0:T(1024)S(1)} %get-tuple-element.868), channel_id=1, replica_groups=mesh['rep'=4,'shard'=4,'seq'=2] {'rep','shard','seq'}, use_global_device_ids=true, to_apply=%region_36.37 | all-reduce | flops 2176 | bytes 17408 | tf_op jit(solution)/shard_map/psum | solution.py:369
  824.0 248.4 %all-reduce.3.cloned.1.call-done = f32[704,3072]{1,0:T(8,128)} async-done(((f32[704,3072]{1,0:T(8,128)}), f32[704,3072]{1,0:T(8,128)}) %all-reduce.3.cloned.1.call-update) | async-done | bytes 8650768 | tf_op jit(solution)/shard_map/psum | solution.py:412
  1072.4 6.3 fusion.79
  (285 shorter events, 83.0 us)
Async XLA Ops:
  7.2 60.3 %copy-start.6 = (bf16[128,1024]{1,0:T(8,128)(2,1)S(1)}, bf16[128,1024]{1,0:T(8,128)(2,1)}, u32[]{:S(2)}) copy-start(bf16[128,1024]{1,0:T(8,128)(2,1)} %param.30) | copy-start | bytes 786436
  7.2 60.3 %copy-start.37 = (f32[1024]{0:T(1024)S(1)}, f32[1024]{0:T(1024)}, u32[]{:S(2)}) copy-start(f32[1024]{0:T(1024)} %param.32) | copy-start | bytes 12292
  7.2 31.9 %all-gather.20.cloned.1.call-start = ((), (), s32[]{:S(2)}) async-start(), calls=%async_computation.9 | async-start | bytes 1310720 | tf_op jit(solution)/shard_map/all_gather | solution.py:105
  7.9 59.5 %all-gather.14.cloned.1.call-start = ((), (), s32[]{:S(2)}) async-start(), calls=%async_computation.6 | async-start | bytes 1310720 | tf_op jit(solution)/shard_map/all_gather | solution.py:104
  8.7 60.6 %copy-start.45 = (f32[64]{0:T(128)S(1)}, f32[64]{0:T(128)}, u32[]{:S(2)}) copy-start(f32[64]{0:T(128)} %param.38) | copy-start | bytes 772
  8.7 95.8 %all-gather.18.cloned.1.call-start = ((), (), s32[]{:S(2)}) async-start(), calls=%async_computation.8 | async-start | bytes 2621440 | tf_op jit(solution)/shard_map/all_gather | solution.py:103
  9.4 120.8 %all-gather.22.cloned.1.call-start = ((), (), s32[]{:S(2)}) async-start(), calls=%async_computation.10 | async-start | bytes 1179648 | tf_op jit(solution)/shard_map/all_gather | solution.py:126
  12.2 92.4 %copy-start.40 = (f32[128]{0:T(128)}, f32[128]{0:T(128)S(1)}, u32[]{:S(2)}) copy-start(f32[128]{0:T(128)S(1)} %add_rsqrt_fusion.3) | copy-start | bytes 1540
  41.5 114.6 %all-gather.16.cloned.1.call-start = ((), (), s32[]{:S(2)}) async-start(), calls=%async_computation.7 | async-start | bytes 1179648 | tf_op jit(solution)/shard_map/all_gather | solution.py:125
  70.1 122.9 %all-gather.24.cloned.1.call-start = ((), (), s32[]{:S(2)}) async-start(), calls=%async_computation.11 | async-start | bytes 2621440 | tf_op jit(solution)/shard_map/all_gather | solution.py:201
  70.7 220.4 %all-gather.26.cloned.1.call-start = ((), (), s32[]{:S(2)}) async-start(), calls=%async_computation.12 | async-start | bytes 11796480 | tf_op jit(solution)/shard_map/all_gather | solution.py:209
  71.4 317.7 %all-gather.28.cloned.1.call-start = ((), (), s32[]{:S(2)}) async-start(), calls=%async_computation.13 | async-start | bytes 11796480 | tf_op jit(solution)/shard_map/all_gather | solution.py:210
  72.2 415.0 %all-gather.30.cloned.1.call-start = ((), (), s32[]{:S(2)}) async-start(), calls=%async_computation.14 | async-start | bytes 11796480 | tf_op jit(solution)/shard_map/all_gather | solution.py:211
  72.9 34.0 %copy-start.43 = (f32[64]{0:T(128)S(1)}, f32[64]{0:T(128)}, u32[]{:S(2)}) copy-start(f32[64]{0:T(128)} %param.37) | copy-start | bytes 772
  72.9 536.0 %reduce-scatter.2.cloned.1.call-start = ((), (), s32[]{:S(2)}) async-start(), calls=%async_computation.15 | async-start | bytes 4718592 | tf_op jit(solution)/shard_map/reduce_scatter | solution.py:325
  168.4 27.2 %copy-start.1 = (bf16[1024,512]{0,1:T(8,128)(2,1)}, bf16[1024,512]{0,1:T(8,128)(2,1)S(1)}, u32[]{:S(2)}) copy-start(bf16[1024,512]{0,1:T(8,128)(2,1)S(1)} %get-tuple-element.1466) | copy-start | bytes 3145732
  168.4 27.1 %copy-start.39 = (f32[1024]{0:T(1024)S(1)}, f32[1024]{0:T(1024)}, u32[]{:S(2)}) copy-start(f32[1024]{0:T(1024)} %param.39) | copy-start | bytes 12292
  168.5 27.0 %copy-start.24 = (bf16[8,2,128,64]{2,3,1,0:T(8,128)(2,1)}, bf16[8,2,128,64]{2,3,1,0:T(8,128)(2,1)S(1)}, u32[]{:S(2)}) copy-start(bf16[8,2,128,64]{2,3,1,0:T(8,128)(2,1)S(1)} %convert_element_type.107) | copy-start | bytes 786436
  195.5 309.3 %copy-start.4 = (f32[128,1024]{1,0:T(8,128)}, f32[128,1024]{1,0:T(8,128)S(1)}, u32[]{:S(2)}) copy-start(f32[128,1024]{1,0:T(8,128)S(1)} %get-tuple-element.1006) | copy-start | bytes 1572868
  195.6 193.5 %copy-start.19 = (bf16[128,1024]{1,0:T(8,128)(2,1)}, bf16[128,1024]{1,0:T(8,128)(2,1)S(1)}, u32[]{:S(2)}) copy-start(bf16[128,1024]{1,0:T(8,128)(2,1)S(1)} %multiply_convert_fusion.4) | copy-start | bytes 786436
  299.3 187.9 %copy-start.31 = (bf16[128,1024]{1,0:T(8,128)(2,1)S(1)}, bf16[128,1024]{1,0:T(8,128)(2,1)}, u32[]{:S(2)}) copy-start(bf16[128,1024]{1,0:T(8,128)(2,1)} %param.43) | copy-start | bytes 786436
  487.2 15.9 %slice-start = ((s8[9437184]{0:T(1024)(128)(4,1)}), s8[1048576]{0:T(1024)(128)(4,1)S(1)}, s32[]{:S(2)}) async-start(s8[9437184]{0:T(1024)(128)(4,1)} %bitcast.268), calls=%async_computation.21 | async-start | bytes 2097152
  487.2 15.9 %slice-start.1 = ((s8[9437184]{0:T(1024)(128)(4,1)}), s8[4194304]{0:T(1024)(128)(4,1)S(1)}, s32[]{:S(2)}) async-start(s8[9437184]{0:T(1024)(128)(4,1)} %bitcast.268), calls=%async_computation.22 | async-start | bytes 8388608
  497.1 6.0 copy-start.10
  497.1 6.0 copy-start.12
  497.1 6.0 slice-start.2
  544.8 5.0 copy-start.2
  544.8 116.0 %all-gather.34.cloned.1.call-start = ((), (), s32[]{:S(2)}) async-start(), calls=%async_computation.17 | async-start | bytes 2359296 | tf_op jit(solution)/shard_map/all_gather | solution.py:382
  545.5 142.2 %all-gather.36.cloned.1.call-start = ((), (), s32[]{:S(2)}) async-start(), calls=%async_computation.18 | async-start | bytes 2359296 | tf_op jit(solution)/shard_map/all_gather | solution.py:383
  546.1 177.3 %all-gather.38.cloned.1.call-start = ((), (), s32[]{:S(2)}) async-start(), calls=%async_computation.19 | async-start | bytes 2359296 | tf_op jit(solution)/shard_map/all_gather | solution.py:384
  546.9 215.5 %all-gather.32.cloned.1.call-start = ((), (), s32[]{:S(2)}) async-start(), calls=%async_computation.16 | async-start | bytes 4718592 | tf_op jit(solution)/shard_map/all_gather | solution.py:381
  549.8 12.2 %copy-start.44 = (f32[64]{0:T(128)S(1)}, f32[64]{0:T(128)}, u32[]{:S(2)}) copy-start(f32[64]{0:T(128)} %param.37) | copy-start | bytes 772
  563.6 46.5 %copy-start.23 = (f32[128,512]{0,1:T(8,128)S(1)}, f32[128,512]{0,1:T(8,128)}, u32[]{:S(2)}) copy-start(f32[128,512]{0,1:T(8,128)} %copy-done.22) | copy-start | bytes 786436
  563.7 46.5 %copy-start.47 = (f32[64]{0:T(128)S(1)}, f32[64]{0:T(128)}, u32[]{:S(2)}) copy-start(f32[64]{0:T(128)} %param.38) | copy-start | bytes 772
  564.1 47.5 %copy-start.28 = (f32[128,512]{1,0:T(8,128)S(1)}, f32[128,512]{1,0:T(8,128)}, u32[]{:S(2)}) copy-start(f32[128,512]{1,0:T(8,128)} %copy-done.27) | copy-start | bytes 786436
  564.1 47.5 %copy-start.30 = (f32[128,512]{1,0:T(8,128)S(1)}, f32[128,512]{1,0:T(8,128)}, u32[]{:S(2)}) copy-start(f32[128,512]{1,0:T(8,128)} %copy.95) | copy-start | bytes 786436
  610.4 6.4 copy-start.13
  613.4 12.6 %all-to-all-start.1 = ((bf16[128,8,128]{2,0,1:T(8,128)(2,1)}), bf16[128,8,128]{2,0,1:T(8,128)(2,1)S(1)}, u32[]{:S(2)}, u32[]{:S(2)}) async-start(bf16[128,8,128]{2,0,1:T(8,128)(2,1)} %bitcast.256), calls=%async_computation.2 | async-start | bytes 524288 | tf_op jit(solution)/shard_map/all_to_all | solution.py:376
  616.8 14.1 %copy-start.11 = (bf16[128,4608]{1,0:T(8,128)(2,1)S(1)}, bf16[128,4608]{1,0:T(8,128)(2,1)}, u32[]{:S(2)}) copy-start(bf16[128,4608]{1,0:T(8,128)(2,1)} %copy-done.10) | copy-start | bytes 3538948
  626.7 25.7 %all-to-all-start.3 = ((bf16[128,8,576]{0,2,1:T(8,128)(2,1)}), bf16[128,8,576]{0,2,1:T(8,128)(2,1)}, u32[]{:S(2)}, u32[]{:S(2)}) async-start(bf16[128,8,576]{0,2,1:T(8,128)(2,1)} %bitcast.281), calls=%async_computation.4 | async-start | bytes 2359296 | tf_op jit(solution)/shard_map/all_to_all | solution.py:378
  631.0 26.0 %copy-start.8 = (bf16[128,4608]{1,0:T(8,128)(2,1)S(1)}, bf16[128,4608]{1,0:T(8,128)(2,1)}, u32[]{:S(2)}) copy-start(bf16[128,4608]{1,0:T(8,128)(2,1)} %get-tuple-element.985) | copy-start | bytes 3538948
  652.4 40.1 %all-to-all-start.2 = ((bf16[128,8,576]{0,2,1:T(8,128)(2,1)}), bf16[128,8,576]{0,2,1:T(8,128)(2,1)}, u32[]{:S(2)}, u32[]{:S(2)}) async-start(bf16[128,8,576]{0,2,1:T(8,128)(2,1)} %bitcast.280), calls=%async_computation.3 | async-start | bytes 2359296 | tf_op jit(solution)/shard_map/all_to_all | solution.py:377
  656.9 3.9 copy-start.34
  692.5 23.7 %all-to-all-start.4 = ((bf16[128,8,576]{0,2,1:T(8,128)(2,1)}), bf16[128,8,576]{0,2,1:T(8,128)(2,1)}, u32[]{:S(2)}, u32[]{:S(2)}) async-start(bf16[128,8,576]{0,2,1:T(8,128)(2,1)} %bitcast.70), calls=%async_computation.5 | async-start | bytes 2359296 | tf_op jit(solution)/shard_map/all_to_all | solution.py:379
  696.8 4.9 copy-start.21
  716.3 11.9 %all-to-all-start = ((bf16[128,8,128]{2,0,1:T(8,128)(2,1)}), bf16[128,8,128]{2,0,1:T(8,128)(2,1)S(1)}, u32[]{:S(2)}, u32[]{:S(2)}) async-start(bf16[128,8,128]{2,0,1:T(8,128)(2,1)} %bitcast.257), calls=%async_computation.1 | async-start | bytes 524288 | tf_op jit(solution)/shard_map/all_to_all | solution.py:375
  719.7 352.7 %all-reduce.3.cloned.1.call-start = ((), (), s32[]{:S(2)}) async-start(), calls=%async_computation.20 | async-start | bytes 17301504 | tf_op jit(solution)/shard_map/psum | solution.py:412
  773.0 49.9 %copy-start.16 = (f32[128,1024]{1,0:T(8,128)S(1)}, f32[128,1024]{1,0:T(8,128)}, u32[]{:S(2)}) copy-start(f32[128,1024]{1,0:T(8,128)} %copy-done.15) | copy-start | bytes 1572868
  (27 other events, 59.2 us)
Sparse Core Ops, SparseCore 0:
  9.9 29.2 all-gather.19
  40.9 26.4 all-gather.13
  69.3 35.1 all-gather.17
  106.9 23.3 all-gather.21
  132.6 23.4 all-gather.15
  157.8 35.1 all-gather.23
  194.8 96.1 all-gather.25
  292.9 96.1 all-gather.27
  391.0 96.1 all-gather.29
  544.9 64.0 reduce-scatter.1
  610.9 37.9 all-gather.33
  650.6 37.1 all-gather.35
  689.7 33.7 all-gather.37
  725.8 36.5 all-gather.31
  772.1 300.2 all-reduce.2
where the time goes:
time: 1100 us; the launch traced here: 1090 us
  waiting for transfers between devices  832 us (76%)
  matrix products  94.4 us (9%)
  local copies, waits for them, and re-layouts  46.5 us (4%)
  blocking collectives  43.9 us (4%)
  other arithmetic  25.5 us (2%)
  starting transfers between devices  20.4 us (2%)
  between operations  15.4 us (1%)
  loops' own time  11.8 us (1%)
    psum x1, waiting for transfers between devices, local(): own_grads = lax.psum(group_grads, 'rep')  248 us
    all_gather x1, waiting for transfers between devices, local(): gate_rows = lax.all_gather(w_gate, 'shard', axis=0, tiled=True)  95.4 us
    all_gather x1, waiting for transfers between devices, local(): down_rows = lax.all_gather(w_down, 'shard', axis=0, tiled=True)  89.8 us
    all_gather x1, waiting for transfers between devices, local(): up_rows = lax.all_gather(w_up, 'shard', axis=0, tiled=True)  89.8 us
    reduce_scatter x1, waiting for transfers between devices, local(): lax.psum_scatter(lax.map(one_block, starts).reshape(row_count * lax.axis_...  44.8 us
    psum x1, blocking collectives, local(): lax.psum((attn_gain_part, mlp_gain_part, query_gain_part, key_gain_part),...  43.9 us
    all_gather x1, waiting for transfers between devices, local(): lax.all_gather(attn_grads, ('shard', 'seq'), axis=0, tiled=True)  34.2 us
    all_gather x1, waiting for transfers between devices, local(): lax.all_gather(w_query, 'shard', axis=0, tiled=True)  31.4 us
  transfers between devices with their start and end apart: 20, of which 17 were waited for; matrix products, arithmetic and copies ran while one was open for 9% of the time, Pallas kernels for 0%

commit v1 on v0

--- a/solution.py
+++ b/solution.py
@@ -1,6 +1,8 @@
 import jax
 import jax.numpy as jnp
 from jax import lax
+from jax.experimental import pallas as pl
+from jax.experimental.pallas import tpu as pltpu
 from jax.sharding import PartitionSpec as P
 
 norm_eps = 1e-05
@@ -436,6 +438,522 @@
     )
 
 
+group_axes = ("shard", "seq")
+
+
+def group_swap(values, mask):
+    return lax.ppermute(values, group_axes, [(rank, rank ^ mask) for rank in range(8)])
+
+
+def rep_swap(values, mask):
+    return lax.ppermute(values, "rep", [(rank, rank ^ mask) for rank in range(4)])
+
+
+def rep_shift(values, step):
+    pairs = [(rank, rank + step) for rank in range(4) if 0 <= rank + step < 4]
+    return lax.ppermute(values, "rep", pairs)
+
+
+def gather_pieces(own):
+    same_core = [own] + [group_swap(own, mask) for mask in (2, 4, 6)]
+    other_core = [group_swap(piece, 1) for piece in same_core]
+    return [piece for pair in zip(same_core, other_core) for piece in pair]
+
+
+def place_pieces(pieces, rank, axis):
+    shape = list(pieces[0].shape)
+    width = shape[axis]
+    shape[axis] = width * len(pieces)
+    whole = jnp.zeros(shape, pieces[0].dtype)
+    for mask, piece in enumerate(pieces):
+        whole = lax.dynamic_update_slice_in_dim(whole, piece, (rank ^ mask) * width, axis)
+    return whole
+
+
+def add_rounded(left, right):
+    return (left.astype(jnp.float32) + right.astype(jnp.float32)).astype(jnp.bfloat16)
+
+
+def scatter_sum(partial, rank, axis=0):
+    width = partial.shape[axis] // 8
+
+    def block(mask):
+        return lax.dynamic_slice_in_dim(partial, (rank ^ mask) * width, width, axis)
+
+    halves = [
+        add_rounded(block(mask), group_swap(block(mask ^ 1).astype(jnp.bfloat16), 1))
+        for mask in (0, 2, 4, 6)
+    ]
+    moved = [group_swap(half, mask) for mask, half in zip((2, 4, 6), halves[1:])]
+    total = halves[0].astype(jnp.float32)
+    for piece in moved:
+        total = total + piece.astype(jnp.float32)
+    return total
+
+
+def rep_chain_sum(values, chunk_count):
+    place = lax.axis_index("rep")
+    rows = values.shape[0] // chunk_count
+    chunks = values.reshape(chunk_count, rows, values.shape[1])
+
+    def own(index):
+        return lax.dynamic_index_in_dim(
+            chunks, jnp.clip(index, 0, chunk_count - 1), 0, keepdims=False
+        )
+
+    last = 3
+    from_left = []
+    from_right = []
+    for tick in range(chunk_count + 2):
+        up = own(tick - place)
+        down = own(tick - (last - place))
+        if tick:
+            up = add_rounded(up, from_left[-1])
+            down = add_rounded(down, from_right[-1])
+        from_left.append(rep_shift(up, 1))
+        from_right.append(rep_shift(down, -1))
+    left = jnp.stack(from_left)
+    right = jnp.stack(from_right)
+    left = lax.dynamic_slice_in_dim(left, jnp.maximum(place - 1, 0), chunk_count)
+    right = lax.dynamic_slice_in_dim(right, jnp.maximum(last - place - 1, 0), chunk_count)
+    total = (
+        chunks.astype(jnp.float32) + left.astype(jnp.float32) + right.astype(jnp.float32)
+    )
+    return total.reshape(values.shape)
+
+
+def rep_halving_sum(values):
+    place = lax.axis_index("rep")
+    low = place % 2
+    high = place // 2
+    half = values.shape[0] // 2
+    quarter = half // 2
+    kept = lax.dynamic_slice_in_dim(values, low * half, half)
+    sent = lax.dynamic_slice_in_dim(values, (1 - low) * half, half)
+    part = add_rounded(kept, rep_swap(sent, 1))
+    kept = lax.dynamic_slice_in_dim(part, high * quarter, quarter)
+    sent = lax.dynamic_slice_in_dim(part, (1 - high) * quarter, quarter)
+    part = add_rounded(kept, rep_swap(sent, 2))
+    other = rep_swap(part, 2)
+    part = jnp.where(
+        high == 0, jnp.concatenate([part, other]), jnp.concatenate([other, part])
+    )
+    other = rep_swap(part, 1)
+    return jnp.where(low == 0, jnp.concatenate([part, other]), jnp.concatenate([other, part]))
+
+
+def sum_everywhere(values):
+    for mask in (1, 2, 4):
+        values = values + group_swap(values, mask)
+    for mask in (1, 2):
+        values = values + rep_swap(values, mask)
+    return values
+
+
+def lower_lanes(shape, width):
+    return lax.broadcasted_iota(jnp.int32, shape, 1) % (2 * width) < width
+
+
+def pair_scale(values, head_dim):
+    lower = lower_lanes(values.shape, head_dim)
+    low = jnp.sum(jnp.where(lower, values, 0.0), axis=1, keepdims=True)
+    high = jnp.sum(jnp.where(lower, 0.0, values), axis=1, keepdims=True)
+    return jnp.where(lower, low, high) * (1.0 / head_dim)
+
+
+def swap_halves(values, head_dim):
+    width = values.shape[1]
+    half = head_dim // 2
+    return jnp.where(
+        lower_lanes(values.shape, half),
+        pltpu.roll(values, width - half, 1),
+        pltpu.roll(values, half, 1),
+    )
+
+
+def rotated_heads(raw, query_gain, key_gain, cosine, sine, head_dim):
+    width = 2 * head_dim
+    queries = raw[:, :width]
+    keys = raw[:, width:]
+    query_norm = lax.rsqrt(pair_scale(queries * queries, head_dim) + norm_eps)
+    key_norm = lax.rsqrt(pair_scale(keys * keys, head_dim) + norm_eps)
+    query_hat = queries * query_norm
+    key_hat = keys * key_norm
+    scaled = query_hat * query_gain
+    query_rot = scaled * cosine + swap_halves(scaled, head_dim) * sine
+    scaled = key_hat * key_gain
+    key_rot = scaled * cosine + swap_halves(scaled, head_dim) * sine
+    lower = lower_lanes(keys.shape, head_dim)
+    key_twice = jnp.where(lower, key_rot, pltpu.roll(key_rot, head_dim, 1))
+    value_twice = jnp.where(lower, pltpu.roll(keys, head_dim, 1), keys)
+    return query_hat, query_norm, key_hat, key_norm, query_rot, key_twice, value_twice
+
+
+def stack_heads(values, head_dim):
+    lower = lower_lanes(values.shape, head_dim)
+    zero = jnp.zeros_like(values)
+    return jnp.concatenate(
+        [jnp.where(lower, values, zero), jnp.where(lower, zero, values)], axis=0
+    )
+
+
+def join_heads(stacked, head_dim):
+    rows = stacked.shape[0] // 2
+    lower = lower_lanes((rows, stacked.shape[1]), head_dim)
+    return jnp.where(lower, stacked[:rows], stacked[rows:])
+
+
+def allowed_pairs(doc_column, doc_row, first, rows, span):
+    row_index = first + lax.broadcasted_iota(jnp.int32, (rows, span), 0)
+    key_index = lax.broadcasted_iota(jnp.int32, (rows, span), 1)
+    return (doc_column == doc_row) & (key_index <= row_index)
+
+
+def dot_last(left, right):
+    return lax.dot_general(left, right, contract_last, preferred_element_type=jnp.float32)
+
+
+def dot_first(left, right):
+    return lax.dot_general(left, right, contract_first, preferred_element_type=jnp.float32)
+
+
+def dot_plain(left, right):
+    return jnp.dot(left, right, preferred_element_type=jnp.float32)
+
+
+def attention_forward(head_dim, block):
+    score_scale = head_dim ** (-0.5)
+    width = 2 * head_dim
+
+    def kernel(
+        x_ref, gain_ref, weight_ref, query_gain_ref, key_gain_ref, cos_ref, sin_ref,
+        doc_col_ref, doc_row_ref, mix_ref, normed_ref, raw_ref, lse_ref,
+        query_scr, key_scr, value_scr,
+    ):
+        total = x_ref.shape[0]
+        for first in range(0, total, block):
+            rows = pl.ds(first, block)
+            x = x_ref[rows, :].astype(jnp.float32)
+            normed = (x * rms_scale(x) * gain_ref[...]).astype(jnp.bfloat16)
+            normed_ref[rows, :] = normed
+            raw = dot_plain(normed, weight_ref[...])
+            raw_ref[rows, :] = raw
+            parts = rotated_heads(
+                raw, query_gain_ref[...], key_gain_ref[...], cos_ref[rows, :], sin_ref[rows, :],
+                head_dim,
+            )
+            query_scr[rows, :] = parts[4].astype(jnp.bfloat16)
+            key_scr[rows, :] = parts[5].astype(jnp.bfloat16)
+            value_scr[rows, :] = parts[6].astype(jnp.bfloat16)
+        for first in range(0, total, block):
+            rows = pl.ds(first, block)
+            span = first + block
+            stacked = stack_heads(query_scr[rows, :], head_dim)
+            allowed = allowed_pairs(
+                doc_col_ref[rows, :], doc_row_ref[:, :span], first, block, span
+            )
+            allowed = jnp.concatenate([allowed, allowed], axis=0)
+            scores = dot_last(stacked, key_scr[:span, :]) * score_scale
+            scores = jnp.where(allowed, scores, very_low)
+            high = jnp.max(scores, axis=1, keepdims=True)
+            powers = jnp.exp(scores - high)
+            row_total = jnp.sum(powers, axis=1, keepdims=True)
+            probs = (powers * (1.0 / row_total)).astype(jnp.bfloat16)
+            mixed = dot_plain(probs, value_scr[:span, :])
+            mix_ref[rows, :] = join_heads(mixed, head_dim).astype(jnp.bfloat16)
+            lse_ref[pl.ds(2 * first, 2 * block), :] = high + jnp.log(row_total)
+
+    def call(x, gain, weight, query_gain, key_gain, cosine, sine, doc_column, doc_row):
+        total, model = x.shape
+        return pl.pallas_call(
+            kernel,
+            name="attention_forward",
+            out_shape=(
+                jax.ShapeDtypeStruct((total, width), jnp.bfloat16),
+                jax.ShapeDtypeStruct((total, model), jnp.bfloat16),
+                jax.ShapeDtypeStruct((total, 2 * width), jnp.float32),
+                jax.ShapeDtypeStruct((2 * total, 1), jnp.float32),
+            ),
+            scratch_shapes=[pltpu.VMEM((total, width), jnp.bfloat16)] * 3,
+        )(x, gain, weight, query_gain, key_gain, cosine, sine, doc_column, doc_row)
+
+    return call
+
+
+def attention_backward(head_dim, block):
+    score_scale = head_dim ** (-0.5)
+    width = 2 * head_dim
+
+    def kernel(
+        raw_ref, mix_ref, resid_ref, out_cols_ref, lse_ref, query_gain_ref, key_gain_ref,
+        cos_ref, sin_ref, doc_col_ref, doc_row_ref, grads_ref, query_part_ref, key_part_ref,
+        query_scr, key_scr, value_scr, key_sum, value_sum,
+    ):
+        total = raw_ref.shape[0]
+        query_gain = query_gain_ref[...]
+        key_gain = key_gain_ref[...]
+
+        def heads_of(rows):
+            return rotated_heads(
+                raw_ref[rows, :], query_gain, key_gain, cos_ref[rows, :], sin_ref[rows, :],
+                head_dim,
+            )
+
+        def unrotated(grad, rows):
+            return grad * cos_ref[rows, :] - swap_halves(grad, head_dim) * sin_ref[rows, :]
+
+        def norm_back(upstream, hat, norm, gain):
+            scaled = upstream * gain
+            return norm * (scaled - hat * pair_scale(scaled * hat, head_dim))
+
+        for first in range(0, total, block):
+            rows = pl.ds(first, block)
+            parts = heads_of(rows)
+            query_scr[rows, :] = parts[4].astype(jnp.bfloat16)
+            key_scr[rows, :] = parts[5].astype(jnp.bfloat16)
+            value_scr[rows, :] = parts[6].astype(jnp.bfloat16)
+        key_sum[...] = jnp.zeros_like(key_sum)
+        value_sum[...] = jnp.zeros_like(value_sum)
+        query_part = jnp.zeros((1, width), jnp.float32)
+        for first in range(0, total, block):
+            rows = pl.ds(first, block)
+            span = first + block
+            stacked = stack_heads(query_scr[rows, :], head_dim)
+            mix_grad = dot_plain(resid_ref[rows, :], out_cols_ref[...]).astype(jnp.bfloat16)
+            stacked_grad = stack_heads(mix_grad, head_dim)
+            mixed = mix_ref[rows, :].astype(jnp.float32)
+            delta = jnp.sum(
+                stacked_grad.astype(jnp.float32) * jnp.concatenate([mixed, mixed], axis=0),
+                axis=1,
+                keepdims=True,
+            )
+            allowed = allowed_pairs(
+                doc_col_ref[rows, :], doc_row_ref[:, :span], first, block, span
+            )
+            allowed = jnp.concatenate([allowed, allowed], axis=0)
+            scores = dot_last(stacked, key_scr[:span, :]) * score_scale
+            lse = lse_ref[pl.ds(2 * first, 2 * block), :]
+            probs = jnp.exp(jnp.where(allowed, scores - lse, very_low))
+            prob_grad = dot_last(stacked_grad, value_scr[:span, :])
+            score_grad = (probs * (prob_grad - delta)).astype(jnp.bfloat16)
+            rotated = join_heads(dot_plain(score_grad, key_scr[:span, :]), head_dim)
+            key_sum[:span, :] += dot_first(score_grad, stacked)
+            value_sum[:span, :] += dot_first(probs.astype(jnp.bfloat16), stacked_grad)
+            query_hat, query_norm = heads_of(rows)[:2]
+            straight = unrotated(rotated * score_scale, rows)
+            query_part = query_part + jnp.sum(straight * query_hat, axis=0, keepdims=True)
+            grads_ref[rows, :width] = norm_back(
+                straight, query_hat, query_norm, query_gain
+            ).astype(jnp.bfloat16)
+        key_part = jnp.zeros((1, width), jnp.float32)
+        for first in range(0, total, block):
+            rows = pl.ds(first, block)
+            key_hat, key_norm = heads_of(rows)[2:4]
+            summed = key_sum[rows, :]
+            summed = (summed + pltpu.roll(summed, head_dim, 1)) * score_scale
+            values = value_sum[rows, :]
+            values = values + pltpu.roll(values, head_dim, 1)
+            straight = unrotated(summed, rows)
+            key_part = key_part + jnp.sum(straight * key_hat, axis=0, keepdims=True)
+            key_grad = norm_back(straight, key_hat, key_norm, key_gain)
+            lower = lower_lanes(key_grad.shape, head_dim)
+            grads_ref[rows, width:] = jnp.where(lower, key_grad, values).astype(jnp.bfloat16)
+        query_part_ref[...] = query_part
+        key_part_ref[...] = key_part
+
+    def call(raw, mix, resid, out_cols, lse, query_gain, key_gain, cosine, sine, doc_col, doc_row):
+        total = raw.shape[0]
+        return pl.pallas_call(
+            kernel,
+            name="attention_backward",
+            out_shape=(
+                jax.ShapeDtypeStruct((total, 2 * width), jnp.bfloat16),
+                jax.ShapeDtypeStruct((1, width), jnp.float32),
+                jax.ShapeDtypeStruct((1, width), jnp.float32),
+            ),
+            scratch_shapes=[pltpu.VMEM((total, width), jnp.bfloat16)] * 3
+            + [pltpu.VMEM((total, width), jnp.float32)] * 2,
+        )(raw, mix, resid, out_cols, lse, query_gain, key_gain, cosine, sine, doc_col, doc_row)
+
+    return call
+
+
+def local_by_heads(
+    tokens_in,
+    doc_lengths,
+    attn_gain,
+    w_query,
+    key_weight,
+    value_weight,
+    w_output,
+    query_norm_gain,
+    key_norm_gain,
+    mlp_gain,
+    w_gate,
+    w_up,
+    w_down,
+    out_grad,
+):
+    row_count, model_width = tokens_in.shape
+    head_dim = query_norm_gain.shape[0]
+    query_width = w_query.shape[1]
+    kv_width = key_weight.shape[1]
+    rank_count = 8
+    pair_width = 2 * head_dim
+    total = row_count * rank_count
+    block = 256
+    core = lax.axis_index("seq")
+    shard = lax.axis_index("shard")
+    rank = shard * 2 + core
+
+    x_all = place_pieces(gather_pieces(tokens_in), rank, 0)
+
+    shard_rows = w_query.shape[0]
+    by_head = jnp.concatenate(
+        [
+            w_query.reshape(shard_rows, rank_count, pair_width),
+            key_weight.reshape(shard_rows, rank_count, head_dim),
+            value_weight.reshape(shard_rows, rank_count, head_dim),
+        ],
+        axis=2,
+    )
+
+    def head_columns(mask):
+        picked = lax.dynamic_index_in_dim(by_head, rank ^ mask, 1, keepdims=False)
+        return picked if mask == 0 else group_swap(picked, mask)
+
+    head_weight = jnp.zeros((model_width, 2 * pair_width), jnp.bfloat16)
+    for mask in (0, 2, 4, 6):
+        head_weight = lax.dynamic_update_slice_in_dim(
+            head_weight, head_columns(mask), (shard ^ (mask // 2)) * shard_rows, 0
+        )
+
+    out_part = lax.dynamic_slice_in_dim(w_output, core * row_count, row_count)
+    out_weight = place_pieces(gather_pieces(out_part), rank, 0)
+    grad_all = place_pieces(gather_pieces(out_grad), rank, 0)
+
+    index = jnp.arange(total, dtype=jnp.int32)
+    docs, offsets = doc_info(doc_lengths[0], index)
+    half_dim = head_dim // 2
+    inverse_freq = rope_base ** (-(jnp.arange(half_dim, dtype=jnp.float32) * 2.0 / head_dim))
+    angles = offsets.astype(jnp.float32)[:, None] * inverse_freq[None, :]
+    cosine = jnp.cos(angles)
+    sine = jnp.sin(angles)
+    cosine = jnp.concatenate([cosine] * 4, axis=1)
+    sine = jnp.concatenate([-sine, sine, -sine, sine], axis=1)
+    doc_column = docs[:, None]
+    doc_row = docs[None, :]
+    query_gain = jnp.concatenate([query_norm_gain] * 2)[None, :]
+    key_gain = jnp.concatenate([key_norm_gain] * 2)[None, :]
+
+    mix, normed, raw, lse = attention_forward(head_dim, block)(
+        x_all, attn_gain[None, :], head_weight, query_gain, key_gain, cosine, sine,
+        doc_column, doc_row,
+    )
+    mix_all = place_pieces(gather_pieces(mix), rank, 1)
+
+    x_float = x_all.astype(jnp.float32)
+    residual = x_float + dot_last(mix_all, out_weight)
+    norm_two = rms_scale(residual)
+    resid_hat = residual * norm_two
+    normed_mid = (resid_hat * mlp_gain).astype(jnp.bfloat16)
+
+    hidden_rows = w_gate.shape[0] // 2
+
+    def own_rows(weight):
+        return lax.dynamic_slice_in_dim(weight, core * hidden_rows, hidden_rows)
+
+    gate_rows = own_rows(w_gate)
+    up_rows = own_rows(w_up)
+    down_rows = own_rows(w_down)
+    gate = dot_last(normed_mid, gate_rows)
+    up = dot_last(normed_mid, up_rows)
+    grad_hidden = dot_last(grad_all, down_rows)
+    gate_sig = jax.nn.sigmoid(gate)
+    hidden = (gate * gate_sig * up).astype(jnp.bfloat16)
+    gate_grad = (grad_hidden * up * gate_sig * (1.0 + gate * (1.0 - gate_sig))).astype(jnp.bfloat16)
+    up_grad = (grad_hidden * gate * gate_sig).astype(jnp.bfloat16)
+    mid_part = dot_plain(gate_grad, gate_rows) + dot_plain(up_grad, up_rows)
+    grad_mid = scatter_sum(mid_part, rank)
+
+    own_first = rank * row_count
+
+    def own_tokens(values):
+        return lax.dynamic_slice_in_dim(values, own_first, row_count)
+
+    own_hat = own_tokens(resid_hat)
+    grad_resid = out_grad.astype(jnp.float32) + root_mean_backward(
+        own_hat, own_tokens(norm_two), mlp_gain, grad_mid
+    )
+    mlp_gain_part = jnp.sum(grad_mid * own_hat, axis=0)
+    resid_all = place_pieces(gather_pieces(grad_resid.astype(jnp.bfloat16)), rank, 0)
+
+    act_out = own_tokens(residual) + scatter_sum(dot_plain(hidden, down_rows), rank)
+
+    mlp_grads = jnp.concatenate(
+        [
+            dot_first(gate_grad, normed_mid).astype(jnp.bfloat16),
+            dot_first(up_grad, normed_mid).astype(jnp.bfloat16),
+            dot_first(hidden, grad_all).astype(jnp.bfloat16),
+        ],
+        axis=0,
+    )
+    mlp_sums = rep_chain_sum(mlp_grads, 6)
+
+    out_cols = lax.dynamic_slice_in_dim(out_weight, rank * pair_width, pair_width, 1)
+    head_grads, query_part, key_part = attention_backward(head_dim, block)(
+        raw, mix, resid_all, out_cols, lse, query_gain, key_gain, cosine, sine,
+        doc_column, doc_row,
+    )
+    in_part = dot_last(head_grads, head_weight)
+    x_norm = rms_scale(x_float)
+    attn_gain_part = jnp.sum(in_part * (x_float * x_norm), axis=0)
+    query_gain_part = query_part[0, :head_dim] + query_part[0, head_dim:]
+    gains = sum_everywhere(
+        jnp.concatenate(
+            [attn_gain_part, mlp_gain_part, query_gain_part, key_part[0, :head_dim]]
+        )[None, :]
+    )[0]
+
+    weight_part = dot_first(normed, head_grads).astype(jnp.bfloat16)
+    resid_own = lax.dynamic_slice_in_dim(resid_all, own_first, row_count, 1)
+    out_grads = dot_first(resid_own, mix_all).astype(jnp.bfloat16)
+
+    def weight_block(mask):
+        piece = lax.dynamic_slice_in_dim(weight_part, (rank ^ mask) * row_count, row_count)
+        return piece if mask == 0 else group_swap(piece, mask)
+
+    attn_grads = place_pieces([weight_block(mask) for mask in range(rank_count)], rank, 1)
+    attn_grads = jnp.concatenate([attn_grads, out_grads], axis=1)
+    attn_grads = rep_halving_sum(attn_grads).astype(jnp.float32)
+
+    grad_in_norm = scatter_sum(in_part, rank)
+    own_x = tokens_in.astype(jnp.float32)
+    own_norm = rms_scale(own_x)
+    in_grad = grad_resid + root_mean_backward(own_x * own_norm, own_norm, attn_gain, grad_in_norm)
+
+    by_rank = attn_grads[:, : 2 * query_width].reshape(row_count, rank_count, 2 * pair_width)
+    grad_query = by_rank[:, :, :pair_width].reshape(row_count, query_width)
+    grad_key = by_rank[:, :, pair_width : pair_width + head_dim].reshape(row_count, kv_width)
+    grad_value = by_rank[:, :, pair_width + head_dim :].reshape(row_count, kv_width)
+    grad_output = attn_grads[:, 2 * query_width :]
+    return (
+        act_out,
+        in_grad,
+        gains[:model_width],
+        grad_query,
+        grad_key,
+        grad_value,
+        grad_output,
+        gains[2 * model_width : 2 * model_width + head_dim],
+        gains[2 * model_width + head_dim :],
+        gains[model_width : 2 * model_width],
+        mlp_sums[:hidden_rows],
+        mlp_sums[hidden_rows : 2 * hidden_rows],
+        mlp_sums[2 * hidden_rows :],
+    )
+
+
 def solution(mesh):
     placed = (
         P(("rep", "shard", "seq"), None),
@@ -453,8 +971,10 @@
         P("shard", None),
         P(("rep", "shard", "seq"), None),
     )
+    sizes = dict(mesh.shape)
+    by_heads = sizes["rep"] == 4 and sizes["shard"] == 4 and sizes["seq"] == 2
     return jax.shard_map(
-        local,
+        local_by_heads if by_heads else local,
         mesh=mesh,
         in_specs=placed,
         out_specs=(

time: 1100 us -> 408 us (0.37)
  waiting for transfers between devices: 832 us -> 76.6 us
  starting transfers between devices: 20.4 us -> 122 us
  local copies, waits for them, and re-layouts: 46.5 us -> 112 us
  matrix products: 94.4 us -> 30 us
  blocking collectives: 43.9 us -> 0 us
  Pallas kernels: 0 us -> 22.2 us
  between operations: 15.4 us -> 2.01 us
  other arithmetic: 25.5 us -> 37.4 us
  loops' own time: 11.8 us -> 0 us
    all_gather x13 -> x0, waiting for transfers between devices: 493 us -> none  [the longest x1 95.4 us: local(): gate_rows = lax.all_gather(w_gate, 'shard', axis=0, tiled=True)]
    psum x1 -> x0, waiting for transfers between devices: 248 us -> none  [local(): own_grads = lax.psum(group_grads, 'rep')]
    ppermute x0 -> x91, starting transfers between devices: none -> 122 us  [the longest x16 56.8 us: rep_shift(): return lax.ppermute(values, 'rep', pairs)]
    ppermute x0 -> x91, waiting for transfers between devices: none -> 76.6 us  [the longest x69 48.9 us: group_swap(): lax.ppermute(values, group_axes, [(rank, rank ^ mask) for rank in range(8)])]
    dot_general x26 -> x13, matrix products: 94.4 us -> 30 us  [the longest x5 15.6 us: dot_last(): lax.dot_general(left, right, contract_last, preferred_element_type=jnp.fl...]
    reduce_scatter x1 -> x0, waiting for transfers between devices: 44.8 us -> none  [local(): lax.psum_scatter(lax.map(one_block, starts).reshape(row_count * lax.axis_...]
    psum x1 -> x0, blocking collectives: 43.9 us -> none  [local(): lax.psum((attn_gain_part, mlp_gain_part, query_gain_part, key_gain_part),...]
    all_to_all x5 -> x0, waiting for transfers between devices: 39.4 us -> none  [the longest x1 20 us: local(): lax.all_to_all(up_grad_store, ('shard', 'seq'), split_axis=1, concat_axis...]
  transfers between devices with their start and end apart: 20 -> 91, of which waited for: 17 -> 26; matrix products, arithmetic and copies ran while one was open for 9% -> 36% of each run, Pallas kernels for 0% -> 6%
where the time goes in v1:
time: 408 us; the launch traced here: 403 us
  starting transfers between devices  122 us (30%)
  local copies, waits for them, and re-layouts  112 us (27%)
  waiting for transfers between devices  76.6 us (19%)
  other arithmetic  37.4 us (9%)
  matrix products  30 us (7%)
  Pallas kernels  22.2 us (5%)
    ppermute x16, starting transfers between devices, rep_shift(): return lax.ppermute(values, 'rep', pairs)  56.8 us
    ppermute x69, starting transfers between devices, group_swap(): lax.ppermute(values, group_axes, [(rank, rank ^ mask) for rank in range(8)])  51.7 us
    ppermute x69, waiting for transfers between devices, group_swap(): lax.ppermute(values, group_axes, [(rank, rank ^ mask) for rank in range(8)])  48.9 us
    dynamic_update_slice x47, local copies, waits for them, and re-layouts, place_pieces(): lax.dynamic_update_slice_in_dim(whole, piece, (rank ^ mask) * width, axis)  36.9 us
    unnamed x109, local copies, waits for them, and re-layouts  31.2 us
    ppermute x16, waiting for transfers between devices, rep_shift(): return lax.ppermute(values, 'rep', pairs)  19.9 us
    dot_general x5, matrix products, dot_last(): lax.dot_general(left, right, contract_last, preferred_element_type=jnp.fl...  15.6 us
    ppermute x6, starting transfers between devices, rep_swap(): lax.ppermute(values, 'rep', [(rank, rank ^ mask) for rank in range(4)])  14 us
  transfers between devices with their start and end apart: 91, of which 26 were waited for; matrix products, arithmetic and copies ran while one was open for 36% of the time, Pallas kernels for 6%

profile of v1, /device:TPU:0, one launch (start us, length us, event | category | flops | bytes accessed | tf_op | source)
XLA Modules:
  0.0 402.7 jit_solution(3467815839577982414)
XLA Ops:
  1.2 2.6 collective-permute-start.1
  8.8 2.0 copy_bitcast_fusion
  18.0 3.2 fusion.39
  28.2 2.9 collective-permute-start.9
  32.1 2.1 collective-permute-done.9
  34.3 2.9 collective-permute-start.5
  43.4 7.2 %collective-permute-done.18 = bf16[128,1024]{1,0:T(8,128)(2,1)} collective-permute-done((bf16[128,1024]{1,0:T(8,128)(2,1)}, bf16[128,1024]{1,0:T(8,128)(2,1)}, u32[]{:S(2)}, u32[]{:S(2)}) %collective-permute-start.18) | collective-permute-done | bytes 262176 | tf_op jit(solution)/shard_map/ppermute | solution.py:445
  53.0 2.9 collective-permute-start.22
  62.7 10.3 %collective-permute-done.20 = bf16[128,1024]{1,0:T(8,128)(2,1)} collective-permute-done((bf16[128,1024]{1,0:T(8,128)(2,1)}, bf16[128,1024]{1,0:T(8,128)(2,1)}, u32[]{:S(2)}, u32[]{:S(2)}) %collective-permute-start.20) | collective-permute-done | bytes 262176 | tf_op jit(solution)/shard_map/ppermute | solution.py:445
  74.2 2.1 fusion
  76.3 10.3 %attention_forward.1 = (bf16[1024,128]{1,0:T(8,128)(2,1)}, bf16[1024,1024]{1,0:T(8,128)(2,1)}, f32[1024,256]{1,0:T(8,128)}, f32[2048,1]{1,0:T(8,128)}) custom-call(bf16[1024,1024]{1,0:T(8,128)(2,1)} %constant_dynamic-update-slice_fusion.43.x_ref, f32[1,1024]{1,0:T(1,128)} %bitcast.162, bf16[1024,256]{1,0:T(8,128)(2,1)} %copy-done.7, ...), custom_call_target="tpu_custom_call" | custom-call | tf_op jit(solution)/shard_map/attention_forward/pallas_call | solution.py:668
  98.8 3.7 collective-permute-done.11
  102.6 7.1 %collective-permute-done.13 = bf16[1024,128]{1,0:T(8,128)(2,1)S(1)} collective-permute-done((bf16[1024,128]{1,0:T(8,128)(2,1)S(1)}, bf16[1024,128]{1,0:T(8,128)(2,1)S(1)}, u32[]{:S(2)}, u32[]{:S(2)}) %collective-permute-start.13) | collective-permute-done | bytes 262176 | tf_op jit(solution)/shard_map/ppermute | solution.py:445
  111.7 5.1 %multiply_reduce_fusion = (f32[1024]{0:T(1024)S(1)}, f32[1024,1024]{1,0:T(8,128)S(1)}) fusion(bf16[1024,1024]{1,0:T(8,128)(2,1)S(1)} %constant_dynamic-update-slice_fusion.32, bf16[1024,1024]{1,0:T(8,128)(2,1)S(1)} %constant_dynamic-update-slice_fusion.24, bf16[1024,1024]{1,0:T(8,128)(2,1)} %constant_dynamic-update-slice_fusion.43.x_ref), kind=kOutput, calls=%fused_computation.8 | convolution fusion | flops 2151676928 | bytes 10489856 | tf_op jit(solution)/shard_map/dot_general | solution.py:613
  122.1 2.4 multiply_convert_fusion.1
  138.9 2.0 collective-permute-start.42
  143.9 5.0 %collective-permute-done.44 = bf16[128,1024]{1,0:T(8,128)(2,1)S(1)} collective-permute-done((bf16[128,1024]{1,0:T(8,128)(2,1)S(1)}, bf16[128,1024]{1,0:T(8,128)(2,1)S(1)}, u32[]{:S(2)}, u32[]{:S(2)}) %collective-permute-start.44) | collective-permute-done | bytes 262176 | tf_op jit(solution)/shard_map/ppermute | solution.py:445
  149.0 3.5 collective-permute-start.75
  159.7 3.3 collective-permute-done.30
  163.0 3.9 collective-permute-done.28
  166.9 2.1 collective-permute-start.46
  177.0 4.6 %collective-permute-start.76 = (bf16[288,1024]{1,0:T(8,128)(2,1)}, bf16[288,1024]{1,0:T(8,128)(2,1)}, u32[]{:S(2)}, u32[]{:S(2)}) collective-permute-start(bf16[288,1024]{1,0:T(8,128)(2,1)} %get-tuple-element.118), channel_id=1, source_target_pairs={{0,8},{8,16},{16,24},{1,9},{9,17},{17,25},{2,10},{10,18},{18,26},{... | collective-permute-start | bytes 1769480 | tf_op jit(solution)/shard_map/ppermute | solution.py:454
  188.1 11.9 %attention_backward.1 = (bf16[1024,256]{1,0:T(8,128)(2,1)}, f32[1,128]{1,0:T(1,128)}, f32[1,128]{1,0:T(1,128)}) custom-call(f32[1024,256]{1,0:T(8,128)} %get-tuple-element.21.raw_ref, bf16[1024,128]{1,0:T(8,128)(2,1)} %get-tuple-element.20.mix_ref, bf16[1024,1024]{1,0:T(8,128)(2,1)} %constant_dynamic-update-slice_fusion.8.resid_ref, ...), custom_call_target="tpu_custom_call" | custom-call | tf_op jit(solution)/shard_map/attention_backward/pallas_call | solution.py:766
  202.4 5.2 %fusion.2 = (f32[1024]{0:T(1024)}, f32[1024,1024]{1,0:T(8,128)}) fusion(bf16[1024,1024]{1,0:T(8,128)(2,1)} %constant_dynamic-update-slice_fusion.43.x_ref, f32[1024]{0:T(1024)S(1)} %add_rsqrt_fusion, bf16[1024,256]{1,0:T(8,128)(2,1)} %get-tuple-element.23, bf16[1024,256]{1,0:T(8,128)(2,1)} %copy-done.7), kind=kOutput, calls=%fused_computation.6 | convolution fusion | flops 541064192 | bytes 7348224 | tf_op jit(solution)/shard_map/dot_general | solution.py:613
  208.5 2.6 dynamic-slice_convert_fusion.3
  212.8 2.5 convolution_convert_fusion.3
  216.5 2.1 convolution_convert_fusion.4
  223.8 2.7 collective-permute-start.63
  264.6 2.0 bitcast_dynamic-update-slice_fusion.14
  274.2 4.6 %collective-permute-start.77 = (bf16[288,1024]{1,0:T(8,128)(2,1)S(1)}, bf16[288,1024]{1,0:T(8,128)(2,1)S(1)}, u32[]{:S(2)}, u32[]{:S(2)}) collective-permute-start(bf16[288,1024]{1,0:T(8,128)(2,1)S(1)} %get-tuple-element.116), channel_id=1, source_target_pairs={{0,8},{8,16},{16,24},{1,9},{9,17},{17,25},{2,10},{10,18},{18,26},{... | collective-permute-start | bytes 1769480 | tf_op jit(solution)/shard_map/ppermute | solution.py:454
  279.6 2.9 collective-permute-start.72
  284.5 2.1 fusion.34
  286.6 7.8 %collective-permute-done.72 = bf16[32,3072]{1,0:T(8,128)(2,1)S(1)} collective-permute-done((bf16[32,3072]{1,0:T(8,128)(2,1)S(1)}, bf16[32,3072]{1,0:T(8,128)(2,1)S(1)}, u32[]{:S(2)}, u32[]{:S(2)}) %collective-permute-start.72) | collective-permute-done | bytes 196640 | tf_op jit(solution)/shard_map/ppermute | solution.py:449
  294.5 3.5 collective-permute-start.73
  299.8 12.3 %collective-permute-start.78 = (bf16[288,1024]{1,0:T(8,128)(2,1)S(1)}, bf16[288,1024]{1,0:T(8,128)(2,1)S(1)}, u32[]{:S(2)}, u32[]{:S(2)}) collective-permute-start(bf16[288,1024]{1,0:T(8,128)(2,1)S(1)} %get-tuple-element.114), channel_id=1, source_target_pairs={{0,8},{8,16},{16,24},{1,9},{9,17},{17,25},{2,10},{10,18},{18,26},{... | collective-permute-start | bytes 1769480 | tf_op jit(solution)/shard_map/ppermute | solution.py:454
  313.1 2.0 collective-permute-start.74
  315.1 8.1 %collective-permute-done.86 = bf16[288,1024]{1,0:T(8,128)(2,1)S(1)} collective-permute-done((bf16[288,1024]{1,0:T(8,128)(2,1)S(1)}, bf16[288,1024]{1,0:T(8,128)(2,1)S(1)}, u32[]{:S(2)}, u32[]{:S(2)}) %collective-permute-start.86) | collective-permute-done | bytes 589856 | tf_op jit(solution)/shard_map/ppermute | solution.py:454
  327.2 5.9 %collective-permute-start.79 = (bf16[288,1024]{1,0:T(8,128)(2,1)}, bf16[288,1024]{1,0:T(8,128)(2,1)}, u32[]{:S(2)}, u32[]{:S(2)}) collective-permute-start(bf16[288,1024]{1,0:T(8,128)(2,1)} %get-tuple-element.112), channel_id=1, source_target_pairs={{0,8},{8,16},{16,24},{1,9},{9,17},{17,25},{2,10},{10,18},{18,26},{... | collective-permute-start | bytes 1769480 | tf_op jit(solution)/shard_map/ppermute | solution.py:454
  336.3 2.5 copy.96
  341.4 2.7 fusion.12
  345.4 5.9 %collective-permute-start.80 = (bf16[288,1024]{1,0:T(8,128)(2,1)}, bf16[288,1024]{1,0:T(8,128)(2,1)}, u32[]{:S(2)}, u32[]{:S(2)}) collective-permute-start(bf16[288,1024]{1,0:T(8,128)(2,1)} %get-tuple-element.110), channel_id=1, source_target_pairs={{0,8},{8,16},{16,24},{1,9},{9,17},{17,25},{2,10},{10,18},{18,26},{... | collective-permute-start | bytes 1769480 | tf_op jit(solution)/shard_map/ppermute | solution.py:454
  354.8 2.0 copy.97
  360.5 2.0 bitcast_dynamic-update-slice_fusion.4
  367.5 4.6 %collective-permute-start.81 = (bf16[288,1024]{1,0:T(8,128)(2,1)S(1)}, bf16[288,1024]{1,0:T(8,128)(2,1)S(1)}, u32[]{:S(2)}, u32[]{:S(2)}) collective-permute-start(bf16[288,1024]{1,0:T(8,128)(2,1)S(1)} %get-tuple-element.108), channel_id=1, source_target_pairs={{0,8},{8,16},{16,24},{1,9},{9,17},{17,25},{2,10},{10,18},{18,26},{... | collective-permute-start | bytes 1769480 | tf_op jit(solution)/shard_map/ppermute | solution.py:454
  382.4 5.1 %collective-permute-start.82 = (bf16[288,1024]{1,0:T(8,128)(2,1)S(1)}, bf16[288,1024]{1,0:T(8,128)(2,1)S(1)}, u32[]{:S(2)}, u32[]{:S(2)}) collective-permute-start(bf16[288,1024]{1,0:T(8,128)(2,1)S(1)} %get-tuple-element.106), channel_id=1, source_target_pairs={{0,8},{8,16},{16,24},{1,9},{9,17},{17,25},{2,10},{10,18},{18,26},{... | collective-permute-start | bytes 1769480 | tf_op jit(solution)/shard_map/ppermute | solution.py:454
  388.4 3.9 collective-permute-done.90
  394.8 4.5 %convert_add_fusion = f32[6,288,1024]{2,1,0:T(8,128)S(1)} fusion(bf16[6,288,1024]{2,1,0:T(8,128)(2,1)S(1)} %bitcast.148, bf16[8,288,1024]{2,1,0:T(8,128)(2,1)} %bitcast_dynamic-update-slice_fusion, s32[]{:T(128)S(6)} %max.55, bf16[8,288,1024]{2,1,0:T(8,128)(2,1)S(1)} %bitcast_dynamic-update-slice_fusion.8, s32[]{:T(128)S(6)} %max.61), kind=kLoop, calls=%fused_computation | loop fusion | flops 8847360 | bytes 17694728 | tf_op jit(solution)/shard_map/add | solution.py:520
  399.4 3.1 fusion.49
  (394 shorter events, 195.2 us)
Async XLA Ops:
  0.7 36.5 %collective-permute-start = (bf16[128,1024]{1,0:T(8,128)(2,1)}, bf16[128,1024]{1,0:T(8,128)(2,1)}, u32[]{:S(2)}, u32[]{:S(2)}) collective-permute-start(bf16[128,1024]{1,0:T(8,128)(2,1)} %param.14), channel_id=1, source_target_pairs={{0,1},{1,0},{2,3},{3,2},{4,5},{5,4},{6,7},{7,6},{8,9},{9,8},{10,11... | collective-permute-start | bytes 786440 | tf_op jit(solution)/shard_map/ppermute | solution.py:445
  1.2 39.0 %collective-permute-start.1 = (bf16[128,1024]{1,0:T(8,128)(2,1)}, bf16[128,1024]{1,0:T(8,128)(2,1)}, u32[]{:S(2)}, u32[]{:S(2)}) collective-permute-start(bf16[128,1024]{1,0:T(8,128)(2,1)} %param.14), channel_id=1, source_target_pairs={{0,2},{1,3},{2,0},{3,1},{4,6},{5,7},{6,4},{7,5},{8,10},{9,11},{10,... | collective-permute-start | bytes 786440 | tf_op jit(solution)/shard_map/ppermute | solution.py:445
  3.8 49.3 %collective-permute-start.3 = (bf16[128,1024]{1,0:T(8,128)(2,1)}, bf16[128,1024]{1,0:T(8,128)(2,1)}, u32[]{:S(2)}, u32[]{:S(2)}) collective-permute-start(bf16[128,1024]{1,0:T(8,128)(2,1)} %param.14), channel_id=1, source_target_pairs={{0,4},{1,5},{2,6},{3,7},{4,0},{5,1},{6,2},{7,3},{8,12},{9,13},{10,... | collective-permute-start | bytes 786440 | tf_op jit(solution)/shard_map/ppermute | solution.py:445
  14.0 14.2 %collective-permute-start.7 = (bf16[256,256]{1,0:T(8,128)(2,1)}, bf16[256,256]{1,0:T(8,128)(2,1)}, u32[]{:S(2)}, u32[]{:S(2)}) collective-permute-start(bf16[256,256]{1,0:T(8,128)(2,1)} %get-tuple-element.126), channel_id=1, source_target_pairs={{0,2},{1,3},{2,0},{3,1},{4,6},{5,7},{6,4},{7,5},{8,10},{9,11},{10,... | collective-permute-start | bytes 393224 | tf_op jit(solution)/shard_map/ppermute | solution.py:445
  14.5 17.5 %collective-permute-start.8 = (bf16[256,256]{1,0:T(8,128)(2,1)}, bf16[256,256]{1,0:T(8,128)(2,1)S(1)}, u32[]{:S(2)}, u32[]{:S(2)}) collective-permute-start(bf16[256,256]{1,0:T(8,128)(2,1)} %get-tuple-element.125), channel_id=1, source_target_pairs={{0,4},{1,5},{2,6},{3,7},{4,0},{5,1},{6,2},{7,3},{8,12},{9,13},{10,... | collective-permute-start | bytes 393224 | tf_op jit(solution)/shard_map/ppermute | solution.py:445
  34.3 22.5 %collective-permute-start.5 = (bf16[128,1024]{1,0:T(8,128)(2,1)S(1)}, bf16[128,1024]{1,0:T(8,128)(2,1)S(1)}, u32[]{:S(2)}, u32[]{:S(2)}) collective-permute-start(bf16[128,1024]{1,0:T(8,128)(2,1)S(1)} %copy-done.10), channel_id=1, source_target_pairs={{0,6},{1,7},{2,4},{3,5},{4,2},{5,3},{6,0},{7,1},{8,14},{9,15},{10,... | collective-permute-start | bytes 786440 | tf_op jit(solution)/shard_map/ppermute | solution.py:445
  37.2 13.4 %collective-permute-start.18 = (bf16[128,1024]{1,0:T(8,128)(2,1)}, bf16[128,1024]{1,0:T(8,128)(2,1)}, u32[]{:S(2)}, u32[]{:S(2)}) collective-permute-start(bf16[128,1024]{1,0:T(8,128)(2,1)} %get-tuple-element.78), channel_id=1, source_target_pairs={{0,2},{1,3},{2,0},{3,1},{4,6},{5,7},{6,4},{7,5},{8,10},{9,11},{10,... | collective-permute-start | bytes 786440 | tf_op jit(solution)/shard_map/ppermute | solution.py:445
  39.5 12.8 %collective-permute-start.31 = (bf16[128,1024]{1,0:T(8,128)(2,1)S(1)}, bf16[128,1024]{1,0:T(8,128)(2,1)S(1)}, u32[]{:S(2)}, u32[]{:S(2)}) collective-permute-start(bf16[128,1024]{1,0:T(8,128)(2,1)S(1)} %copy-done.19), channel_id=1, source_target_pairs={{0,1},{1,0},{2,3},{3,2},{4,5},{5,4},{6,7},{7,6},{8,9},{9,8},{10,11... | collective-permute-start | bytes 786440 | tf_op jit(solution)/shard_map/ppermute | solution.py:445
  40.2 15.7 %collective-permute-start.32 = (bf16[128,1024]{1,0:T(8,128)(2,1)S(1)}, bf16[128,1024]{1,0:T(8,128)(2,1)S(1)}, u32[]{:S(2)}, u32[]{:S(2)}) collective-permute-start(bf16[128,1024]{1,0:T(8,128)(2,1)S(1)} %copy-done.19), channel_id=1, source_target_pairs={{0,2},{1,3},{2,0},{3,1},{4,6},{5,7},{6,4},{7,5},{8,10},{9,11},{10,... | collective-permute-start | bytes 786440 | tf_op jit(solution)/shard_map/ppermute | solution.py:445
  52.3 20.7 %collective-permute-start.20 = (bf16[128,1024]{1,0:T(8,128)(2,1)}, bf16[128,1024]{1,0:T(8,128)(2,1)}, u32[]{:S(2)}, u32[]{:S(2)}) collective-permute-start(bf16[128,1024]{1,0:T(8,128)(2,1)} %get-tuple-element.78), channel_id=1, source_target_pairs={{0,4},{1,5},{2,6},{3,7},{4,0},{5,1},{6,2},{7,3},{8,12},{9,13},{10,... | collective-permute-start | bytes 786440 | tf_op jit(solution)/shard_map/ppermute | solution.py:445
  53.0 35.1 %collective-permute-start.22 = (bf16[128,1024]{1,0:T(8,128)(2,1)}, bf16[128,1024]{1,0:T(8,128)(2,1)}, u32[]{:S(2)}, u32[]{:S(2)}) collective-permute-start(bf16[128,1024]{1,0:T(8,128)(2,1)} %get-tuple-element.78), channel_id=1, source_target_pairs={{0,6},{1,7},{2,4},{3,5},{4,2},{5,3},{6,0},{7,1},{8,14},{9,15},{10,... | collective-permute-start | bytes 786440 | tf_op jit(solution)/shard_map/ppermute | solution.py:445
  56.7 31.5 %collective-permute-start.34 = (bf16[128,1024]{1,0:T(8,128)(2,1)S(1)}, bf16[128,1024]{1,0:T(8,128)(2,1)S(1)}, u32[]{:S(2)}, u32[]{:S(2)}) collective-permute-start(bf16[128,1024]{1,0:T(8,128)(2,1)S(1)} %copy-done.19), channel_id=1, source_target_pairs={{0,4},{1,5},{2,6},{3,7},{4,0},{5,1},{6,2},{7,3},{8,12},{9,13},{10,... | collective-permute-start | bytes 786440 | tf_op jit(solution)/shard_map/ppermute | solution.py:445
  57.3 15.7 %collective-permute-start.6 = (bf16[128,1024]{1,0:T(8,128)(2,1)S(1)}, bf16[128,1024]{1,0:T(8,128)(2,1)S(1)}, u32[]{:S(2)}, u32[]{:S(2)}) collective-permute-start(bf16[128,1024]{1,0:T(8,128)(2,1)S(1)} %collective-permute-done.5), channel_id=1, source_target_pairs={{0,1},{1,0},{2,3},{3,2},{4,5},{5,4},{6,7},{7,6},{8,9},{9,8},{10,11... | collective-permute-start | bytes 786440 | tf_op jit(solution)/shard_map/ppermute | solution.py:445
  59.8 28.9 %collective-permute-start.36 = (bf16[128,1024]{1,0:T(8,128)(2,1)S(1)}, bf16[128,1024]{1,0:T(8,128)(2,1)}, u32[]{:S(2)}, u32[]{:S(2)}) collective-permute-start(bf16[128,1024]{1,0:T(8,128)(2,1)S(1)} %copy-done.19), channel_id=1, source_target_pairs={{0,6},{1,7},{2,4},{3,5},{4,2},{5,3},{6,0},{7,1},{8,14},{9,15},{10,... | collective-permute-start | bytes 786440 | tf_op jit(solution)/shard_map/ppermute | solution.py:445
  73.0 15.8 %collective-permute-start.19 = (bf16[128,1024]{1,0:T(8,128)(2,1)}, bf16[128,1024]{1,0:T(8,128)(2,1)}, u32[]{:S(2)}, u32[]{:S(2)}) collective-permute-start(bf16[128,1024]{1,0:T(8,128)(2,1)} %collective-permute-done.18), channel_id=1, source_target_pairs={{0,1},{1,0},{2,3},{3,2},{4,5},{5,4},{6,7},{7,6},{8,9},{9,8},{10,11... | collective-permute-start | bytes 786440 | tf_op jit(solution)/shard_map/ppermute | solution.py:445
  73.0 18.2 %collective-permute-start.21 = (bf16[128,1024]{1,0:T(8,128)(2,1)}, bf16[128,1024]{1,0:T(8,128)(2,1)}, u32[]{:S(2)}, u32[]{:S(2)}) collective-permute-start(bf16[128,1024]{1,0:T(8,128)(2,1)} %collective-permute-done.20), channel_id=1, source_target_pairs={{0,1},{1,0},{2,3},{3,2},{4,5},{5,4},{6,7},{7,6},{8,9},{9,8},{10,11... | collective-permute-start | bytes 786440 | tf_op jit(solution)/shard_map/ppermute | solution.py:445
  88.8 13.8 %collective-permute-start.37 = (bf16[128,1024]{1,0:T(8,128)(2,1)}, bf16[128,1024]{1,0:T(8,128)(2,1)S(1)}, u32[]{:S(2)}, u32[]{:S(2)}) collective-permute-start(bf16[128,1024]{1,0:T(8,128)(2,1)} %collective-permute-done.36), channel_id=1, source_target_pairs={{0,1},{1,0},{2,3},{3,2},{4,5},{5,4},{6,7},{7,6},{8,9},{9,8},{10,11... | collective-permute-start | bytes 786440 | tf_op jit(solution)/shard_map/ppermute | solution.py:445
  91.2 18.5 %collective-permute-start.10 = (bf16[1024,128]{1,0:T(8,128)(2,1)S(1)}, bf16[1024,128]{1,0:T(8,128)(2,1)S(1)}, u32[]{:S(2)}, u32[]{:S(2)}) collective-permute-start(bf16[1024,128]{1,0:T(8,128)(2,1)S(1)} %copy-done.27), channel_id=1, source_target_pairs={{0,1},{1,0},{2,3},{3,2},{4,5},{5,4},{6,7},{7,6},{8,9},{9,8},{10,11... | collective-permute-start | bytes 786440 | tf_op jit(solution)/shard_map/ppermute | solution.py:445
  95.7 14.0 %collective-permute-start.13 = (bf16[1024,128]{1,0:T(8,128)(2,1)S(1)}, bf16[1024,128]{1,0:T(8,128)(2,1)S(1)}, u32[]{:S(2)}, u32[]{:S(2)}) collective-permute-start(bf16[1024,128]{1,0:T(8,128)(2,1)S(1)} %copy-done.27), channel_id=1, source_target_pairs={{0,4},{1,5},{2,6},{3,7},{4,0},{5,1},{6,2},{7,3},{8,12},{9,13},{10,... | collective-permute-start | bytes 786440 | tf_op jit(solution)/shard_map/ppermute | solution.py:445
  96.3 13.6 %collective-permute-start.15 = (bf16[1024,128]{1,0:T(8,128)(2,1)S(1)}, bf16[1024,128]{1,0:T(8,128)(2,1)S(1)}, u32[]{:S(2)}, u32[]{:S(2)}) collective-permute-start(bf16[1024,128]{1,0:T(8,128)(2,1)S(1)} %copy-done.27), channel_id=1, source_target_pairs={{0,6},{1,7},{2,4},{3,5},{4,2},{5,3},{6,0},{7,1},{8,14},{9,15},{10,... | collective-permute-start | bytes 786440 | tf_op jit(solution)/shard_map/ppermute | solution.py:445
  137.7 18.8 %collective-permute-start.24 = (bf16[128,1024]{1,0:T(8,128)(2,1)S(1)}, bf16[128,1024]{1,0:T(8,128)(2,1)S(1)}, u32[]{:S(2)}, u32[]{:S(2)}) collective-permute-start(bf16[128,1024]{1,0:T(8,128)(2,1)S(1)} %get-tuple-element.99), channel_id=1, source_target_pairs={{0,1},{1,0},{2,3},{3,2},{4,5},{5,4},{6,7},{7,6},{8,9},{9,8},{10,11... | collective-permute-start | bytes 786440 | tf_op jit(solution)/shard_map/ppermute | solution.py:445
  138.9 14.0 %collective-permute-start.42 = (bf16[128,1024]{1,0:T(8,128)(2,1)S(1)}, bf16[128,1024]{1,0:T(8,128)(2,1)S(1)}, u32[]{:S(2)}, u32[]{:S(2)}) collective-permute-start(bf16[128,1024]{1,0:T(8,128)(2,1)S(1)} %get-tuple-element.98), channel_id=1, source_target_pairs={{0,4},{1,5},{2,6},{3,7},{4,0},{5,1},{6,2},{7,3},{8,12},{9,13},{10,... | collective-permute-start | bytes 786440 | tf_op jit(solution)/shard_map/ppermute | solution.py:445
  140.8 13.2 %collective-permute-start.40 = (bf16[128,1024]{1,0:T(8,128)(2,1)S(1)}, bf16[128,1024]{1,0:T(8,128)(2,1)S(1)}, u32[]{:S(2)}, u32[]{:S(2)}) collective-permute-start(bf16[128,1024]{1,0:T(8,128)(2,1)S(1)} %get-tuple-element.96), channel_id=1, source_target_pairs={{0,2},{1,3},{2,0},{3,1},{4,6},{5,7},{6,4},{7,5},{8,10},{9,11},{10,... | collective-permute-start | bytes 786440 | tf_op jit(solution)/shard_map/ppermute | solution.py:445
  142.6 27.7 %collective-permute-start.83 = (bf16[288,1024]{1,0:T(8,128)(2,1)S(1)}, bf16[288,1024]{1,0:T(8,128)(2,1)S(1)}, u32[]{:S(2)}, u32[]{:S(2)}) collective-permute-start(bf16[288,1024]{1,0:T(8,128)(2,1)S(1)} %get-tuple-element.121), channel_id=1, source_target_pairs={{8,0},{16,8},{24,16},{9,1},{17,9},{25,17},{10,2},{18,10},{26,18},{... | collective-permute-start | bytes 1769480 | tf_op jit(solution)/shard_map/ppermute | solution.py:454
  149.0 22.6 %collective-permute-start.75 = (bf16[288,1024]{1,0:T(8,128)(2,1)S(1)}, bf16[288,1024]{1,0:T(8,128)(2,1)S(1)}, u32[]{:S(2)}, u32[]{:S(2)}) collective-permute-start(bf16[288,1024]{1,0:T(8,128)(2,1)S(1)} %get-tuple-element.120), channel_id=1, source_target_pairs={{0,8},{8,16},{16,24},{1,9},{9,17},{17,25},{2,10},{10,18},{18,26},{... | collective-permute-start | bytes 1769480 | tf_op jit(solution)/shard_map/ppermute | solution.py:454
  154.0 12.9 %collective-permute-start.28 = (bf16[128,1024]{1,0:T(8,128)(2,1)S(1)}, bf16[128,1024]{1,0:T(8,128)(2,1)S(1)}, u32[]{:S(2)}, u32[]{:S(2)}) collective-permute-start(bf16[128,1024]{1,0:T(8,128)(2,1)S(1)} %get-tuple-element.105), channel_id=1, source_target_pairs={{0,4},{1,5},{2,6},{3,7},{4,0},{5,1},{6,2},{7,3},{8,12},{9,13},{10,... | collective-permute-start | bytes 786440 | tf_op jit(solution)/shard_map/ppermute | solution.py:445
  156.6 12.4 %collective-permute-start.26 = (bf16[128,1024]{1,0:T(8,128)(2,1)S(1)}, bf16[128,1024]{1,0:T(8,128)(2,1)S(1)}, u32[]{:S(2)}, u32[]{:S(2)}) collective-permute-start(bf16[128,1024]{1,0:T(8,128)(2,1)S(1)} %get-tuple-element.103), channel_id=1, source_target_pairs={{0,2},{1,3},{2,0},{3,1},{4,6},{5,7},{6,4},{7,5},{8,10},{9,11},{10,... | collective-permute-start | bytes 786440 | tf_op jit(solution)/shard_map/ppermute | solution.py:445
  163.0 14.0 %collective-permute-start.45 = (bf16[128,1024]{1,0:T(8,128)(2,1)S(1)}, bf16[128,1024]{1,0:T(8,128)(2,1)S(1)}, u32[]{:S(2)}, u32[]{:S(2)}) collective-permute-start(bf16[128,1024]{1,0:T(8,128)(2,1)S(1)} %get-tuple-element.73), channel_id=1, source_target_pairs={{0,1},{1,0},{2,3},{3,2},{4,5},{5,4},{6,7},{7,6},{8,9},{9,8},{10,11... | collective-permute-start | bytes 786440 | tf_op jit(solution)/shard_map/ppermute | solution.py:445
  169.0 13.6 %collective-permute-start.48 = (bf16[128,1024]{1,0:T(8,128)(2,1)S(1)}, bf16[128,1024]{1,0:T(8,128)(2,1)S(1)}, u32[]{:S(2)}, u32[]{:S(2)}) collective-permute-start(bf16[128,1024]{1,0:T(8,128)(2,1)S(1)} %get-tuple-element.73), channel_id=1, source_target_pairs={{0,4},{1,5},{2,6},{3,7},{4,0},{5,1},{6,2},{7,3},{8,12},{9,13},{10,... | collective-permute-start | bytes 786440 | tf_op jit(solution)/shard_map/ppermute | solution.py:445
  170.3 13.7 %collective-permute-start.50 = (bf16[128,1024]{1,0:T(8,128)(2,1)S(1)}, bf16[128,1024]{1,0:T(8,128)(2,1)S(1)}, u32[]{:S(2)}, u32[]{:S(2)}) collective-permute-start(bf16[128,1024]{1,0:T(8,128)(2,1)S(1)} %get-tuple-element.73), channel_id=1, source_target_pairs={{0,6},{1,7},{2,4},{3,5},{4,2},{5,3},{6,0},{7,1},{8,14},{9,15},{10,... | collective-permute-start | bytes 786440 | tf_op jit(solution)/shard_map/ppermute | solution.py:445
  173.0 86.0 %collective-permute-start.84 = (bf16[288,1024]{1,0:T(8,128)(2,1)}, bf16[288,1024]{1,0:T(8,128)(2,1)}, u32[]{:S(2)}, u32[]{:S(2)}) collective-permute-start(bf16[288,1024]{1,0:T(8,128)(2,1)} %get-tuple-element.119), channel_id=1, source_target_pairs={{8,0},{16,8},{24,16},{9,1},{17,9},{25,17},{10,2},{18,10},{26,18},{... | collective-permute-start | bytes 1769480 | tf_op jit(solution)/shard_map/ppermute | solution.py:454
  177.0 82.6 %collective-permute-start.76 = (bf16[288,1024]{1,0:T(8,128)(2,1)}, bf16[288,1024]{1,0:T(8,128)(2,1)}, u32[]{:S(2)}, u32[]{:S(2)}) collective-permute-start(bf16[288,1024]{1,0:T(8,128)(2,1)} %get-tuple-element.118), channel_id=1, source_target_pairs={{0,8},{8,16},{16,24},{1,9},{9,17},{17,25},{2,10},{10,18},{18,26},{... | collective-permute-start | bytes 1769480 | tf_op jit(solution)/shard_map/ppermute | solution.py:454
  211.1 55.5 %collective-permute-start.53 = (bf16[128,1024]{1,0:T(8,128)(2,1)}, bf16[128,1024]{1,0:T(8,128)(2,1)}, u32[]{:S(2)}, u32[]{:S(2)}) collective-permute-start(bf16[128,1024]{1,0:T(8,128)(2,1)} %get-tuple-element.88), channel_id=1, source_target_pairs={{0,1},{1,0},{2,3},{3,2},{4,5},{5,4},{6,7},{7,6},{8,9},{9,8},{10,11... | collective-permute-start | bytes 786440 | tf_op jit(solution)/shard_map/ppermute | solution.py:445
  251.3 16.7 %collective-permute-start.57 = (bf16[128,1024]{1,0:T(8,128)(2,1)}, bf16[128,1024]{1,0:T(8,128)(2,1)}, u32[]{:S(2)}, u32[]{:S(2)}) collective-permute-start(bf16[128,1024]{1,0:T(8,128)(2,1)} %get-tuple-element.86), channel_id=1, source_target_pairs={{0,1},{1,0},{2,3},{3,2},{4,5},{5,4},{6,7},{7,6},{8,9},{9,8},{10,11... | collective-permute-start | bytes 786440 | tf_op jit(solution)/shard_map/ppermute | solution.py:445
  253.5 14.5 %collective-permute-start.55 = (bf16[128,1024]{1,0:T(8,128)(2,1)}, bf16[128,1024]{1,0:T(8,128)(2,1)}, u32[]{:S(2)}, u32[]{:S(2)}) collective-permute-start(bf16[128,1024]{1,0:T(8,128)(2,1)} %get-tuple-element.87), channel_id=1, source_target_pairs={{0,1},{1,0},{2,3},{3,2},{4,5},{5,4},{6,7},{7,6},{8,9},{9,8},{10,11... | collective-permute-start | bytes 786440 | tf_op jit(solution)/shard_map/ppermute | solution.py:445
  259.0 15.1 %collective-permute-start.52 = (bf16[128,1024]{1,0:T(8,128)(2,1)}, bf16[128,1024]{1,0:T(8,128)(2,1)S(1)}, u32[]{:S(2)}, u32[]{:S(2)}) collective-permute-start(bf16[128,1024]{1,0:T(8,128)(2,1)} %get-tuple-element.85), channel_id=1, source_target_pairs={{0,1},{1,0},{2,3},{3,2},{4,5},{5,4},{6,7},{7,6},{8,9},{9,8},{10,11... | collective-permute-start | bytes 786440 | tf_op jit(solution)/shard_map/ppermute | solution.py:445
  266.6 31.4 %collective-permute-start.85 = (bf16[288,1024]{1,0:T(8,128)(2,1)S(1)}, bf16[288,1024]{1,0:T(8,128)(2,1)S(1)}, u32[]{:S(2)}, u32[]{:S(2)}) collective-permute-start(bf16[288,1024]{1,0:T(8,128)(2,1)S(1)} %get-tuple-element.117), channel_id=1, source_target_pairs={{8,0},{16,8},{24,16},{9,1},{17,9},{25,17},{10,2},{18,10},{26,18},{... | collective-permute-start | bytes 1769480 | tf_op jit(solution)/shard_map/ppermute | solution.py:454
  271.0 13.1 %collective-permute-start.56 = (bf16[128,1024]{1,0:T(8,128)(2,1)S(1)}, bf16[128,1024]{1,0:T(8,128)(2,1)S(1)}, u32[]{:S(2)}, u32[]{:S(2)}) collective-permute-start(bf16[128,1024]{1,0:T(8,128)(2,1)S(1)} %get-tuple-element.91), channel_id=1, source_target_pairs={{0,4},{1,5},{2,6},{3,7},{4,0},{5,1},{6,2},{7,3},{8,12},{9,13},{10,... | collective-permute-start | bytes 786440 | tf_op jit(solution)/shard_map/ppermute | solution.py:445
  274.2 23.8 %collective-permute-start.77 = (bf16[288,1024]{1,0:T(8,128)(2,1)S(1)}, bf16[288,1024]{1,0:T(8,128)(2,1)S(1)}, u32[]{:S(2)}, u32[]{:S(2)}) collective-permute-start(bf16[288,1024]{1,0:T(8,128)(2,1)S(1)} %get-tuple-element.116), channel_id=1, source_target_pairs={{0,8},{8,16},{16,24},{1,9},{9,17},{17,25},{2,10},{10,18},{18,26},{... | collective-permute-start | bytes 1769480 | tf_op jit(solution)/shard_map/ppermute | solution.py:454
  279.6 14.8 %collective-permute-start.72 = (bf16[32,3072]{1,0:T(8,128)(2,1)S(1)}, bf16[32,3072]{1,0:T(8,128)(2,1)S(1)}, u32[]{:S(2)}, u32[]{:S(2)}) collective-permute-start(bf16[32,3072]{1,0:T(8,128)(2,1)S(1)} %constant_dynamic-slice_fusion), channel_id=1, source_target_pairs={{0,16},{8,24},{16,0},{24,8},{1,17},{9,25},{17,1},{25,9},{2,18},{10... | collective-permute-start | bytes 589832 | tf_op jit(solution)/shard_map/ppermute | solution.py:449
  294.5 18.5 %collective-permute-start.73 = (bf16[32,3072]{1,0:T(8,128)(2,1)S(1)}, bf16[32,3072]{1,0:T(8,128)(2,1)S(1)}, u32[]{:S(2)}, u32[]{:S(2)}) collective-permute-start(bf16[32,3072]{1,0:T(8,128)(2,1)S(1)} %add_convert_fusion.13), channel_id=1, source_target_pairs={{0,16},{8,24},{16,0},{24,8},{1,17},{9,25},{17,1},{25,9},{2,18},{10... | collective-permute-start | bytes 589832 | tf_op jit(solution)/shard_map/ppermute | solution.py:449
  298.5 24.8 %collective-permute-start.86 = (bf16[288,1024]{1,0:T(8,128)(2,1)S(1)}, bf16[288,1024]{1,0:T(8,128)(2,1)S(1)}, u32[]{:S(2)}, u32[]{:S(2)}) collective-permute-start(bf16[288,1024]{1,0:T(8,128)(2,1)S(1)} %get-tuple-element.115), channel_id=1, source_target_pairs={{8,0},{16,8},{24,16},{9,1},{17,9},{25,17},{10,2},{18,10},{26,18},{... | collective-permute-start | bytes 1769480 | tf_op jit(solution)/shard_map/ppermute | solution.py:454
  299.8 24.6 %collective-permute-start.78 = (bf16[288,1024]{1,0:T(8,128)(2,1)S(1)}, bf16[288,1024]{1,0:T(8,128)(2,1)S(1)}, u32[]{:S(2)}, u32[]{:S(2)}) collective-permute-start(bf16[288,1024]{1,0:T(8,128)(2,1)S(1)} %get-tuple-element.114), channel_id=1, source_target_pairs={{0,8},{8,16},{16,24},{1,9},{9,17},{17,25},{2,10},{10,18},{18,26},{... | collective-permute-start | bytes 1769480 | tf_op jit(solution)/shard_map/ppermute | solution.py:454
  313.1 20.8 %collective-permute-start.74 = (bf16[64,3072]{1,0:T(8,128)(2,1)S(1)}, bf16[64,3072]{1,0:T(8,128)(2,1)S(1)}, u32[]{:S(2)}, u32[]{:S(2)}) collective-permute-start(bf16[64,3072]{1,0:T(8,128)(2,1)S(1)} %maximum_select_fusion.1), channel_id=1, source_target_pairs={{0,8},{8,0},{16,24},{24,16},{1,9},{9,1},{17,25},{25,17},{2,10},{10... | collective-permute-start | bytes 1179656 | tf_op jit(solution)/shard_map/ppermute | solution.py:449
  325.9 14.3 %collective-permute-start.87 = (bf16[288,1024]{1,0:T(8,128)(2,1)}, bf16[288,1024]{1,0:T(8,128)(2,1)}, u32[]{:S(2)}, u32[]{:S(2)}) collective-permute-start(bf16[288,1024]{1,0:T(8,128)(2,1)} %get-tuple-element.113), channel_id=1, source_target_pairs={{8,0},{16,8},{24,16},{9,1},{17,9},{25,17},{10,2},{18,10},{26,18},{... | collective-permute-start | bytes 1769480 | tf_op jit(solution)/shard_map/ppermute | solution.py:454
  327.2 14.2 %collective-permute-start.79 = (bf16[288,1024]{1,0:T(8,128)(2,1)}, bf16[288,1024]{1,0:T(8,128)(2,1)}, u32[]{:S(2)}, u32[]{:S(2)}) collective-permute-start(bf16[288,1024]{1,0:T(8,128)(2,1)} %get-tuple-element.112), channel_id=1, source_target_pairs={{0,8},{8,16},{16,24},{1,9},{9,17},{17,25},{2,10},{10,18},{18,26},{... | collective-permute-start | bytes 1769480 | tf_op jit(solution)/shard_map/ppermute | solution.py:454
  344.1 20.2 %collective-permute-start.88 = (bf16[288,1024]{1,0:T(8,128)(2,1)}, bf16[288,1024]{1,0:T(8,128)(2,1)}, u32[]{:S(2)}, u32[]{:S(2)}) collective-permute-start(bf16[288,1024]{1,0:T(8,128)(2,1)} %get-tuple-element.111), channel_id=1, source_target_pairs={{8,0},{16,8},{24,16},{9,1},{17,9},{25,17},{10,2},{18,10},{26,18},{... | collective-permute-start | bytes 1769480 | tf_op jit(solution)/shard_map/ppermute | solution.py:454
  345.4 18.9 %collective-permute-start.80 = (bf16[288,1024]{1,0:T(8,128)(2,1)}, bf16[288,1024]{1,0:T(8,128)(2,1)}, u32[]{:S(2)}, u32[]{:S(2)}) collective-permute-start(bf16[288,1024]{1,0:T(8,128)(2,1)} %get-tuple-element.110), channel_id=1, source_target_pairs={{0,8},{8,16},{16,24},{1,9},{9,17},{17,25},{2,10},{10,18},{18,26},{... | collective-permute-start | bytes 1769480 | tf_op jit(solution)/shard_map/ppermute | solution.py:454
  (88 other events, 821.1 us)
